TPU v7x, 32 devices: a whole 2x2x4 slice. The times are simulated.
32 devices in a mesh: dp: 4 (over y, core), row: 2 (over x), col: 4 (over z).
Axes of the slice: x: 2, y: 2, z: 4, core: 2. Of those that a mesh axis runs over, the one named last changes fastest.
Arguments:
- x_prompt: bfloat16 [4, 1024, 1536], P('dp', 'col', 'row'), may hold values from -6 to 6
- x_cont: bfloat16 [4, 8, 128, 1536], P('dp', 'col', None, 'row'), may hold values from -6 to 6
- teacher_prompt: bfloat16 [4, 1024, 1536], P('dp', 'col', 'row'), may hold values from -12 to 12
- teacher_cont: bfloat16 [4, 8, 128, 1536], P('dp', 'col', None, 'row'), may hold values from -12 to 12
- segment_ids: int32 [4, 1024], P('dp'), may hold values from 0 to 3, never falling along the last dimension, each value on 1 to 512 neighbouring positions
- offsets: int32 [4, 8], P('dp'), may hold values from 1 to 1024
- prompt_valid: int32 [4, 1024], P('dp', 'col'), may hold values from 0 to 1
- cont_valid: int32 [4, 8, 128], P('dp', 'col'), may hold values from 0 to 1, as said below
- first_gain: bfloat16 [1536], P('row'), may hold values from 0.5 to 1.5
- w_query: bfloat16 [1536, 1536], P('row', 'col'), may hold values from -0.15625 to 0.15625
- w_key: bfloat16 [1536, 1536], P('row', 'col'), may hold values from -0.15625 to 0.15625
- w_value: bfloat16 [1536, 1536], P('row', 'col'), may hold values from -0.15625 to 0.15625
- w_outgate: bfloat16 [1536, 1536], P('row', 'col'), may hold values from -0.15625 to 0.15625
- w_forget: bfloat16 [1536, 24], P('row', 'col'), may hold values from -0.15625 to 0.15625
- forget_bias: float32 [24], P('col'), may hold values from 2.5 to 7.5
- w_out: bfloat16 [1536, 1536], P('col', 'row'), may hold values from -1.75 to 1.75
- second_gain: bfloat16 [1536], P('row'), may hold values from 0.5 to 1.5
- w_gate: bfloat16 [1536, 4096], P('row', 'col'), may hold values from -0.15625 to 0.15625
- w_up: bfloat16 [1536, 4096], P('row', 'col'), may hold values from -0.15625 to 0.15625
- w_down: bfloat16 [4096, 1536], P('col', 'row'), may hold values from -0.09375 to 0.09375
Outputs:
- loss: float32 [], replicated
- grad_prompt: float32 [4, 1024, 1536], P('dp', 'col', 'row')
- grad_cont: float32 [4, 8, 128, 1536], P('dp', 'col', None, 'row')
- grad_first_gain: float32 [1536], P('row')
- grad_query: float32 [1536, 1536], P('row', 'col')
- grad_key: float32 [1536, 1536], P('row', 'col')
- grad_value: float32 [1536, 1536], P('row', 'col')
- grad_outgate: float32 [1536, 1536], P('row', 'col')
- grad_forget: float32 [1536, 24], P('row', 'col')
- grad_forget_bias: float32 [24], P('col')
- grad_out: float32 [1536, 1536], P('col', 'row')
- grad_second_gain: float32 [1536], P('row')
- grad_gate: float32 [1536, 4096], P('row', 'col')
- grad_up: float32 [1536, 4096], P('row', 'col')
- grad_down: float32 [4096, 1536], P('col', 'row')
Inputs may be any that keep to these rules, and one draw needn't show every extreme that they name: `segment_ids`: within a group the document numbers never fall, each document has 1 to 512 positions. `cont_valid`: the first token of every continuation is valid.
All inputs are finite; a program needn't handle non-finite values.
Results may differ from a plain program's by a relative error of at most 0.024.
Values may be sent and summed in bfloat16 or wider, within the bound.
A program may use at most 256 MiB of HBM per device.

v0:
```python
import jax
import jax.numpy as jnp
from jax import lax
from jax.sharding import PartitionSpec as P

D = 1536
HEAD_DIM = 64
PROMPT = 1024
CONTS = 8
CLEN = 128


epsilon = 1e-06
highest = lax.Precision.HIGHEST
masked = -1e30


def matmul(left_op, right_op):
    return jnp.dot(left_op, right_op, preferred_element_type=jnp.float32)


def by_transpose(left_op, right_op):
    return lax.dot_general(
        left_op, right_op, (((1,), (1,)), ((), ())), preferred_element_type=jnp.float32
    )


def inner_rows(left_op, right_op):
    return lax.dot_general(
        left_op, right_op, (((0,), (0,)), ((), ())), preferred_element_type=jnp.float32
    )


def feature_total(partial_sum):
    return lax.psum(partial_sum, "row")


def group_rows(local_rows):
    return lax.all_gather(local_rows, "col", axis=0, tiled=True)


def token_sums(partial_rows):
    return lax.psum_scatter(
        partial_rows.astype(jnp.bfloat16), "col", scatter_dimension=0, tiled=True
    ).astype(jnp.float32)


def row_partials(partial_rows, col_count, blocks, quarter):
    shaped = partial_rows.reshape(
        col_count, blocks, lax.axis_size("row"), quarter, partial_rows.shape[-1]
    )
    return lax.psum_scatter(
        shaped.astype(jnp.bfloat16), "row", scatter_dimension=2, tiled=True
    ).astype(jnp.float32)


def head_rows(own_rows):
    gathered = lax.all_gather(own_rows, "row", axis=2, tiled=True)
    return gathered.reshape(-1, gathered.shape[-1])


def norm_forward(tokens, gain_vec):
    row_total = feature_total(jnp.sum(tokens * tokens, axis=-1))
    factor = lax.rsqrt(row_total / D + epsilon)
    scaled = tokens * factor[:, None]
    return (factor, scaled, (scaled * gain_vec).astype(jnp.bfloat16))


def norm_backward(grad_normed, factor, scaled, gain_vec):
    grad_scaled = grad_normed * gain_vec
    row_total = feature_total(jnp.sum(grad_scaled * scaled, axis=-1))
    gain_grad = jnp.sum(grad_normed * scaled, axis=0)
    return (gain_grad, factor[:, None] * (grad_scaled - scaled * (row_total / D)[:, None]))


def log_total(scores):
    row_top = jnp.max(scores, axis=-1, keepdims=True)
    return row_top + jnp.log(jnp.sum(jnp.exp(scores - row_top), axis=-1, keepdims=True))


def prompt_scores(queries, key_rows, cum_query, cum_key, allowed):
    raw_scores = jnp.einsum("qhd,khd->hqk", queries, key_rows, preferred_element_type=jnp.float32)
    raw_scores = raw_scores * HEAD_DIM ** (-0.5) + cum_query.T[:, :, None] - cum_key.T[:, None, :]
    return jnp.where(allowed[None], raw_scores, masked)


def cont_scores(queries, key_rows, key_cont, cum_query, cum_key, cum_cont, far_ok, near_ok):
    score_scale = HEAD_DIM ** (-0.5)
    query_cum = cum_query.transpose(0, 2, 1)[:, :, :, None]
    far_scores = jnp.einsum("jqhd,khd->jhqk", queries, key_rows, preferred_element_type=jnp.float32)
    far_scores = far_scores * score_scale + query_cum - cum_key.T[None, :, None, :]
    near_scores = jnp.einsum(
        "jqhd,jkhd->jhqk", queries, key_cont, preferred_element_type=jnp.float32
    )
    near_scores = near_scores * score_scale + query_cum - cum_cont.transpose(0, 2, 1)[:, :, None, :]
    far_scores = jnp.where(far_ok[:, None, None, :], far_scores, masked)
    near_scores = jnp.where(near_ok[None, None], near_scores, masked)
    return jnp.concatenate([far_scores, near_scores], axis=-1)


def body(
    x_prompt,
    x_cont,
    teacher_prompt,
    teacher_cont,
    segment_ids,
    offsets,
    prompt_valid,
    cont_valid,
    first_gain,
    w_query,
    w_key,
    w_value,
    w_outgate,
    w_forget,
    forget_bias,
    w_out,
    second_gain,
    w_gate,
    w_up,
    w_down,
):
    row_count = lax.axis_size("row")
    col_count = lax.axis_size("col")
    row_index = lax.axis_index("row")
    local_prompt = x_prompt.shape[1]
    local_conts = x_cont.shape[1]
    quarter = CLEN // row_count
    local_tokens = local_prompt + local_conts * CLEN
    blocks = local_tokens // CLEN
    prompt_blocks = local_prompt // CLEN
    heads_here = w_forget.shape[1]
    width_here = heads_here * HEAD_DIM
    units_here = w_gate.shape[1]
    score_scale = HEAD_DIM ** (-0.5)
    w_project = jnp.concatenate([w_query, w_key, w_value, w_outgate], axis=1)
    w_hidden = jnp.concatenate([w_gate, w_up], axis=1)
    gain_one = first_gain.astype(jnp.float32)
    gain_two = second_gain.astype(jnp.float32)
    position = jnp.arange(PROMPT, dtype=jnp.int32)
    cont_step = jnp.arange(CLEN, dtype=jnp.int32)
    own_step = row_index * quarter + jnp.arange(quarter, dtype=jnp.int32)
    near_ok = cont_step[None, :] <= own_step[:, None]
    own_position = lax.dynamic_index_in_dim(
        position.reshape(col_count, prompt_blocks, row_count, quarter), row_index, 2, keepdims=False
    ).reshape(-1)

    def own_prompt_part(matrix):
        return matrix[:, :prompt_blocks, 0]

    def one_group(carried, group_data):
        (
            acc_project,
            acc_forget,
            acc_bias,
            acc_out,
            acc_hidden,
            acc_down,
            acc_gain_one,
            acc_gain_two,
            error_sum,
            count_sum,
        ) = carried
        (
            prompt_in,
            cont_in,
            teach_prompt,
            teach_cont,
            segment_row,
            offset_row,
            valid_prompt,
            valid_cont,
        ) = group_data
        tokens = jnp.concatenate(
            [prompt_in, cont_in.reshape(local_conts * CLEN, -1)], axis=0
        ).astype(jnp.float32)
        teacher = jnp.concatenate(
            [teach_prompt, teach_cont.reshape(local_conts * CLEN, -1)], axis=0
        ).astype(jnp.float32)
        validity = jnp.concatenate([valid_prompt, valid_cont.reshape(-1)], axis=0).astype(
            jnp.float32
        )
        branch_mask = position[None, :] == offset_row[:, None] - 1
        branch_hot = branch_mask.astype(jnp.float32)
        last_doc = jnp.sum(jnp.where(branch_mask, segment_row[None, :], 0), axis=1)
        far_ok = (position[None, :] < offset_row[:, None]) & (
            segment_row[None, :] == last_doc[:, None]
        )
        own_doc = lax.dynamic_index_in_dim(
            segment_row.reshape(col_count, prompt_blocks, row_count, quarter),
            row_index,
            2,
            keepdims=False,
        ).reshape(-1)
        prompt_ok = (position[None, :] <= own_position[:, None]) & (
            segment_row[None, :] == own_doc[:, None]
        )
        factor_one, scaled_one, normed_one = norm_forward(tokens, gain_one)
        normed_all = group_rows(normed_one)
        project_part = matmul(normed_all, w_project).reshape(
            col_count, blocks, row_count, quarter, 4 * width_here
        )
        forget_part = matmul(normed_all, w_forget).reshape(
            col_count, blocks, row_count, quarter, heads_here
        )
        own_project, own_forget = (
            lax.psum_scatter(project_part, "row", scatter_dimension=2, tiled=True),
            lax.psum_scatter(forget_part, "row", scatter_dimension=2, tiled=True),
        )
        own_query = own_project[..., :width_here].astype(jnp.bfloat16)
        own_kv = own_project[..., width_here : 3 * width_here].astype(jnp.bfloat16)
        gate_logit = own_project[..., 3 * width_here :]
        kv_all, forget_all = (
            lax.all_gather(own_kv, "row", axis=2, tiled=True),
            lax.all_gather(own_forget.astype(jnp.bfloat16), "row", axis=2, tiled=True),
        )
        kv_all = kv_all.reshape(col_count, local_tokens, 2 * width_here)
        pre_gate = (
            forget_all.reshape(col_count, local_tokens, heads_here).astype(jnp.float32)
            + forget_bias
        )
        log_keep = jax.nn.log_sigmoid(pre_gate)
        cum_prompt = jnp.cumsum(log_keep[:, :local_prompt].reshape(PROMPT, heads_here), axis=0)
        branch_cum = jnp.dot(branch_hot, cum_prompt, precision=highest)
        cum_cont = branch_cum[:, None, :] + jnp.cumsum(
            log_keep[:, local_prompt:].reshape(CONTS, CLEN, heads_here), axis=1
        )
        kv_prompt = kv_all[:, :local_prompt].reshape(PROMPT, 2, heads_here, HEAD_DIM)
        key_prompt = kv_prompt[:, 0]
        value_prompt = kv_prompt[:, 1]
        kv_cont = kv_all[:, local_prompt:].reshape(CONTS, CLEN, 2, heads_here, HEAD_DIM)
        key_cont = kv_cont[:, :, 0]
        value_cont = kv_cont[:, :, 1]
        cum_query_prompt = lax.dynamic_index_in_dim(
            cum_prompt.reshape(col_count, prompt_blocks, row_count, quarter, heads_here),
            row_index,
            2,
            keepdims=False,
        ).reshape(-1, heads_here)
        cum_query_cont = lax.dynamic_index_in_dim(
            cum_cont.reshape(CONTS, row_count, quarter, heads_here), row_index, 1, keepdims=False
        )
        query_prompt = own_prompt_part(own_query).reshape(-1, heads_here, HEAD_DIM)
        query_cont = own_query[:, prompt_blocks:, 0].reshape(CONTS, quarter, heads_here, HEAD_DIM)
        scores_prompt = prompt_scores(
            query_prompt, key_prompt, cum_query_prompt, cum_prompt, prompt_ok
        )
        total_prompt = log_total(scores_prompt)
        probs_prompt = jnp.exp(scores_prompt - total_prompt).astype(jnp.bfloat16)
        out_prompt = jnp.einsum(
            "hqk,khd->qhd", probs_prompt, value_prompt, preferred_element_type=jnp.float32
        )
        scores_cont = cont_scores(
            query_cont, key_prompt, key_cont, cum_query_cont, cum_prompt, cum_cont, far_ok, near_ok
        )
        total_cont = log_total(scores_cont)
        probs_cont = jnp.exp(scores_cont - total_cont).astype(jnp.bfloat16)
        out_cont = jnp.einsum(
            "jhqk,khd->jqhd",
            probs_cont[..., :PROMPT],
            value_prompt,
            preferred_element_type=jnp.float32,
        )
        out_cont = out_cont + jnp.einsum(
            "jhqk,jkhd->jqhd",
            probs_cont[..., PROMPT:],
            value_cont,
            preferred_element_type=jnp.float32,
        )
        attended = jnp.concatenate(
            [
                out_prompt.reshape(col_count, prompt_blocks, 1, quarter, width_here),
                out_cont.reshape(col_count, local_conts, 1, quarter, width_here),
            ],
            axis=1,
        )
        gate_sig = jax.nn.sigmoid(gate_logit)
        gated = (attended * gate_sig).astype(jnp.bfloat16)
        gated_all = head_rows(gated)
        residual = tokens + token_sums(matmul(gated_all, w_out))
        factor_two, scaled_two, normed_two = norm_forward(residual, gain_two)
        normed_two_all = group_rows(normed_two)
        hidden_own = row_partials(matmul(normed_two_all, w_hidden), col_count, blocks, quarter)
        gate_rows = hidden_own[..., :units_here]
        up_rows = hidden_own[..., units_here:]
        gate_sig_two = jax.nn.sigmoid(gate_rows)
        silu_rows = gate_rows * gate_sig_two
        hidden_all = head_rows((silu_rows * up_rows).astype(jnp.bfloat16))
        result_rows = residual + token_sums(matmul(hidden_all, w_down))
        deviation = result_rows - teacher
        group_err = 0.5 * jnp.sum(validity[:, None] * deviation * deviation)
        grad_result = validity[:, None] * deviation
        grad_result_all = group_rows(grad_result.astype(jnp.bfloat16))
        grad_down_w = inner_rows(hidden_all, grad_result_all)
        grad_hid = row_partials(by_transpose(grad_result_all, w_down), col_count, blocks, quarter)
        grad_gate = grad_hid * up_rows * gate_sig_two * (1.0 + gate_rows * (1.0 - gate_sig_two))
        grad_up = grad_hid * silu_rows
        grad_hidden_all = head_rows(
            jnp.concatenate([grad_gate, grad_up], axis=-1).astype(jnp.bfloat16)
        )
        grad_hidden_w = inner_rows(normed_two_all, grad_hidden_all)
        grad_normed_two = token_sums(by_transpose(grad_hidden_all, w_hidden))
        gain_two_grad, grad_residual = norm_backward(
            grad_normed_two, factor_two, scaled_two, gain_two
        )
        grad_residual = grad_residual + grad_result
        grad_residual_all = group_rows(grad_residual.astype(jnp.bfloat16))
        grad_out_w = inner_rows(gated_all, grad_residual_all)
        grad_gated = row_partials(
            by_transpose(grad_residual_all, w_out), col_count, blocks, quarter
        )
        grad_attended = (grad_gated * gate_sig).astype(jnp.bfloat16)
        grad_logit = (grad_gated * attended * gate_sig * (1.0 - gate_sig)).astype(jnp.bfloat16)
        grad_att_prompt = own_prompt_part(grad_attended).reshape(-1, heads_here, HEAD_DIM)
        grad_att_cont = grad_attended[:, prompt_blocks:, 0].reshape(
            CONTS, quarter, heads_here, HEAD_DIM
        )
        again_prompt = jnp.exp(
            prompt_scores(query_prompt, key_prompt, cum_query_prompt, cum_prompt, prompt_ok)
            - total_prompt
        )
        grad_prob_prompt = jnp.einsum(
            "qhd,khd->hqk", grad_att_prompt, value_prompt, preferred_element_type=jnp.float32
        )
        grad_score_prompt = (
            again_prompt
            * (grad_prob_prompt - jnp.sum(again_prompt * grad_prob_prompt, axis=-1, keepdims=True))
        ).astype(jnp.bfloat16)
        again_prompt_b = again_prompt.astype(jnp.bfloat16)
        grad_query_prompt = (
            jnp.einsum(
                "hqk,khd->qhd", grad_score_prompt, key_prompt, preferred_element_type=jnp.float32
            )
            * score_scale
        )
        grad_key_prompt = (
            jnp.einsum(
                "hqk,qhd->khd", grad_score_prompt, query_prompt, preferred_element_type=jnp.float32
            )
            * score_scale
        )
        grad_value_prompt = jnp.einsum(
            "hqk,qhd->khd", again_prompt_b, grad_att_prompt, preferred_element_type=jnp.float32
        )
        cum_grad_query_p = jnp.sum(grad_score_prompt, axis=-1, dtype=jnp.float32).T
        cum_grad_key_p = -jnp.sum(grad_score_prompt, axis=1, dtype=jnp.float32).T
        again_cont = jnp.exp(
            cont_scores(
                query_cont,
                key_prompt,
                key_cont,
                cum_query_cont,
                cum_prompt,
                cum_cont,
                far_ok,
                near_ok,
            )
            - total_cont
        )
        grad_prob_cont = jnp.concatenate(
            [
                jnp.einsum(
                    "jqhd,khd->jhqk",
                    grad_att_cont,
                    value_prompt,
                    preferred_element_type=jnp.float32,
                ),
                jnp.einsum(
                    "jqhd,jkhd->jhqk", grad_att_cont, value_cont, preferred_element_type=jnp.float32
                ),
            ],
            axis=-1,
        )
        grad_score_cont = (
            again_cont
            * (grad_prob_cont - jnp.sum(again_cont * grad_prob_cont, axis=-1, keepdims=True))
        ).astype(jnp.bfloat16)
        again_cont_b = again_cont.astype(jnp.bfloat16)
        far_grad = grad_score_cont[..., :PROMPT]
        near_grad = grad_score_cont[..., PROMPT:]
        grad_query_cont = (
            jnp.einsum("jhqk,khd->jqhd", far_grad, key_prompt, preferred_element_type=jnp.float32)
            + jnp.einsum("jhqk,jkhd->jqhd", near_grad, key_cont, preferred_element_type=jnp.float32)
        ) * score_scale
        grad_key_far = (
            jnp.einsum("jhqk,jqhd->khd", far_grad, query_cont, preferred_element_type=jnp.float32)
            * score_scale
        )
        grad_key_near = (
            jnp.einsum("jhqk,jqhd->jkhd", near_grad, query_cont, preferred_element_type=jnp.float32)
            * score_scale
        )
        grad_value_far = jnp.einsum(
            "jhqk,jqhd->khd",
            again_cont_b[..., :PROMPT],
            grad_att_cont,
            preferred_element_type=jnp.float32,
        )
        grad_value_near = jnp.einsum(
            "jhqk,jqhd->jkhd",
            again_cont_b[..., PROMPT:],
            grad_att_cont,
            preferred_element_type=jnp.float32,
        )
        cum_grad_query_c = jnp.sum(grad_score_cont, axis=-1, dtype=jnp.float32).transpose(0, 2, 1)
        cum_grad_key_far = -jnp.sum(far_grad, axis=(0, 2), dtype=jnp.float32).T
        cum_grad_key_near = -jnp.sum(near_grad, axis=2, dtype=jnp.float32).transpose(0, 2, 1)
        kv_grad_prompt = jnp.stack(
            [grad_key_prompt + grad_key_far, grad_value_prompt + grad_value_far], axis=1
        ).reshape(col_count, local_prompt, 2 * width_here)
        kv_grad_cont = jnp.stack([grad_key_near, grad_value_near], axis=2).reshape(
            col_count, local_conts * CLEN, 2 * width_here
        )
        kv_grad_part = jnp.concatenate([kv_grad_prompt, kv_grad_cont], axis=1)
        query_place = lax.dynamic_update_slice_in_dim(
            jnp.zeros((col_count, prompt_blocks, row_count, quarter, heads_here), jnp.float32),
            cum_grad_query_p.reshape(col_count, prompt_blocks, 1, quarter, heads_here),
            row_index,
            axis=2,
        ).reshape(PROMPT, heads_here)
        cont_place = lax.dynamic_update_slice_in_dim(
            jnp.zeros((CONTS, row_count, quarter, heads_here), jnp.float32),
            cum_grad_query_c.reshape(CONTS, 1, quarter, heads_here),
            row_index,
            axis=1,
        ).reshape(CONTS, CLEN, heads_here)
        cum_grad_part = jnp.concatenate(
            [
                (cum_grad_key_p + cum_grad_key_far + query_place).reshape(
                    col_count, local_prompt, heads_here
                ),
                (cum_grad_key_near + cont_place).reshape(col_count, local_conts * CLEN, heads_here),
            ],
            axis=1,
        )
        kv_grad_full, cum_grad_full = lax.psum((kv_grad_part, cum_grad_part), "row")
        cum_grad_cont = cum_grad_full[:, local_prompt:].reshape(CONTS, CLEN, heads_here)
        cum_grad_prompt = cum_grad_full[:, :local_prompt].reshape(PROMPT, heads_here)
        cum_grad_prompt = cum_grad_prompt + jnp.dot(
            branch_hot.T, jnp.sum(cum_grad_cont, axis=1), precision=highest
        )
        log_grad_prompt = lax.cumsum(cum_grad_prompt, axis=0, reverse=True)
        log_grad_cont = lax.cumsum(cum_grad_cont, axis=1, reverse=True)
        log_grad = jnp.concatenate(
            [
                log_grad_prompt.reshape(col_count, local_prompt, heads_here),
                log_grad_cont.reshape(col_count, local_conts * CLEN, heads_here),
            ],
            axis=1,
        )
        pre_grad = log_grad * jax.nn.sigmoid(-pre_gate)
        bias_grad = jnp.sum(pre_grad, axis=(0, 1))
        forget_grad_b = pre_grad.reshape(-1, heads_here).astype(jnp.bfloat16)
        query_grad_own = jnp.concatenate(
            [
                grad_query_prompt.reshape(col_count, prompt_blocks, 1, quarter, width_here),
                grad_query_cont.reshape(col_count, local_conts, 1, quarter, width_here),
            ],
            axis=1,
        )
        qg_grad_all = head_rows(
            jnp.concatenate([query_grad_own.astype(jnp.bfloat16), grad_logit], axis=-1)
        )
        kv_grad_rows = kv_grad_full.reshape(-1, 2 * width_here).astype(jnp.bfloat16)
        project_grad_rows = jnp.concatenate(
            [qg_grad_all[:, :width_here], kv_grad_rows, qg_grad_all[:, width_here:]], axis=-1
        )
        grad_project_w = inner_rows(normed_all, project_grad_rows)
        grad_forget_w = inner_rows(normed_all, forget_grad_b)
        grad_normed_one = token_sums(
            by_transpose(project_grad_rows, w_project) + by_transpose(forget_grad_b, w_forget)
        )
        gain_one_grad, grad_tokens = norm_backward(
            grad_normed_one, factor_one, scaled_one, gain_one
        )
        grad_tokens = grad_tokens + grad_residual
        grad_prompt_one = grad_tokens[:local_prompt]
        grad_cont_one = grad_tokens[local_prompt:].reshape(local_conts, CLEN, -1)
        group_count = jnp.sum(validity) * (row_index == 0).astype(jnp.float32)
        new_carry = (
            acc_project + grad_project_w,
            acc_forget + grad_forget_w,
            acc_bias + bias_grad,
            acc_out + grad_out_w,
            acc_hidden + grad_hidden_w,
            acc_down + grad_down_w,
            acc_gain_one + gain_one_grad,
            acc_gain_two + gain_two_grad,
            error_sum + group_err,
            count_sum + group_count,
        )
        return (new_carry, (grad_prompt_one, grad_cont_one))

    start = (
        jnp.zeros(w_project.shape, jnp.float32),
        jnp.zeros(w_forget.shape, jnp.float32),
        jnp.zeros(forget_bias.shape, jnp.float32),
        jnp.zeros(w_out.shape, jnp.float32),
        jnp.zeros(w_hidden.shape, jnp.float32),
        jnp.zeros(w_down.shape, jnp.float32),
        jnp.zeros(first_gain.shape, jnp.float32),
        jnp.zeros(second_gain.shape, jnp.float32),
        jnp.zeros((), jnp.float32),
        jnp.zeros((), jnp.float32),
    )
    finished, (grad_prompt, grad_cont) = lax.scan(
        one_group,
        start,
        (
            x_prompt,
            x_cont,
            teacher_prompt,
            teacher_cont,
            segment_ids,
            offsets,
            prompt_valid,
            cont_valid,
        ),
    )
    (
        acc_project,
        acc_forget,
        acc_bias,
        acc_out,
        acc_hidden,
        acc_down,
        acc_gain_one,
        acc_gain_two,
        error_sum,
        count_sum,
    ) = finished
    acc_project, acc_forget, acc_bias, acc_out, acc_hidden, acc_down = (
        lax.psum(acc_project.astype(jnp.bfloat16), "dp").astype(jnp.float32),
        lax.psum(acc_forget.astype(jnp.bfloat16), "dp").astype(jnp.float32),
        lax.psum(acc_bias.astype(jnp.bfloat16), "dp").astype(jnp.float32),
        lax.psum(acc_out.astype(jnp.bfloat16), "dp").astype(jnp.float32),
        lax.psum(acc_hidden.astype(jnp.bfloat16), "dp").astype(jnp.float32),
        lax.psum(acc_down.astype(jnp.bfloat16), "dp").astype(jnp.float32),
    )
    gain_one_total, gain_two_total = lax.psum((acc_gain_one, acc_gain_two), ("dp", "col"))
    error_total, count_total = lax.psum((error_sum, count_sum), ("dp", "row", "col"))
    grad_scale = x_prompt.shape[0] * lax.axis_size("dp") * (PROMPT + CONTS * CLEN) / count_total
    loss_value = error_total / (D * count_total)
    width_here = w_query.shape[1]
    units_here = w_gate.shape[1]
    return (
        loss_value,
        grad_prompt * grad_scale,
        grad_cont * grad_scale,
        gain_one_total * grad_scale,
        acc_project[:, :width_here] * grad_scale,
        acc_project[:, width_here : 2 * width_here] * grad_scale,
        acc_project[:, 2 * width_here : 3 * width_here] * grad_scale,
        acc_project[:, 3 * width_here :] * grad_scale,
        acc_forget * grad_scale,
        acc_bias * grad_scale,
        acc_out * grad_scale,
        gain_two_total * grad_scale,
        acc_hidden[:, :units_here] * grad_scale,
        acc_hidden[:, units_here:] * grad_scale,
        acc_down * grad_scale,
    )


def solution(mesh):
    in_specs = (
        P("dp", "col", "row"),
        P("dp", "col", None, "row"),
        P("dp", "col", "row"),
        P("dp", "col", None, "row"),
        P("dp", None),
        P("dp", None),
        P("dp", "col"),
        P("dp", "col", None),
        P("row"),
        P("row", "col"),
        P("row", "col"),
        P("row", "col"),
        P("row", "col"),
        P("row", "col"),
        P("col"),
        P("col", "row"),
        P("row"),
        P("row", "col"),
        P("row", "col"),
        P("col", "row"),
    )
    out_specs = (
        P(),
        P("dp", "col", "row"),
        P("dp", "col", None, "row"),
        P("row"),
        P("row", "col"),
        P("row", "col"),
        P("row", "col"),
        P("row", "col"),
        P("row", "col"),
        P("col"),
        P("col", "row"),
        P("row"),
        P("row", "col"),
        P("row", "col"),
        P("col", "row"),
    )
    return jax.shard_map(body, mesh=mesh, in_specs=in_specs, out_specs=out_specs, check_vma=False)
```

profile of v0, /device:TPU:0, one launch (start us, length us, event | category | flops | bytes accessed | tf_op | source)
XLA Modules:
  0.0 2117.0 jit_solution(3175176937826299997)
XLA Ops:
  22.0 61.6 %all-gather.10.cloned.1.call-done = bf16[2048,768]{1,0:T(8,128)(2,1)} async-done(((bf16[512,768]{1,0:T(8,128)(2,1)}), bf16[2048,768]{1,0:T(8,128)(2,1)}) %all-gather.10.cloned.1.call-update) | async-done | bytes 3145744 | tf_op jit(solution)/shard_map/while/body/eval_jaxpr/all_gather | solution.py:39
  83.6 10.0 fusion.128
  96.0 284.4 %all-reduce.17.cloned.1.call-done = f32[4,4,2,64,1536]{4,3,2,1,0:T(8,128)} async-done(((f32[4,4,2,64,1536]{4,3,2,1,0:T(8,128)}), f32[4,4,2,64,1536]{4,3,2,1,0:T(8,128)}) %all-reduce.17.cloned.1.call-update) | async-done | bytes 12582928
  393.0 9.2 all-reduce.1
  412.3 23.3 %fusion.126 = f32[8,128,6]{2,0,1:T(8,128)S(1)} fusion(f32[8,128,6]{2,0,1:T(8,128)S(1)} %copy.253), kind=kOutput, calls=%fused_computation.242 | output fusion | flops 780288 | bytes 49152 | tf_op jit(solution)/shard_map/while/body/eval_jaxpr/jit(cumsum)/reduce_window_sum | solution.py:225
  506.9 28.6 %all-gather.14.cloned.1.call-done = bf16[4,4,2,64,384]{4,3,1,0,2:T(8,128)(2,1)} async-done(((bf16[4,4,1,64,384]{4,3,1,0,2:T(8,128)(2,1)}), bf16[4,4,2,64,384]{4,3,1,0,2:T(8,128)(2,1)}) %all-gather.14.cloned.1.call-update) | async-done | bytes 1572880 | tf_op jit(solution)/shard_map/while/body/eval_jaxpr/all_gather | solution.py:58
  542.5 59.8 %reduce-scatter.17.cloned.1.call-done = bf16[512,768]{1,0:T(8,128)(2,1)} async-done(((bf16[2048,768]{1,0:T(8,128)(2,1)}), bf16[512,768]{1,0:T(8,128)(2,1)}) %reduce-scatter.17.cloned.1.call-update) | async-done | bytes 786448 | tf_op jit(solution)/shard_map/while/body/eval_jaxpr/reduce_scatter | solution.py:43
  615.1 59.6 %all-gather.16.cloned.1.call-done = bf16[2048,768]{1,0:T(8,128)(2,1)} async-done(((bf16[512,768]{1,0:T(8,128)(2,1)}), bf16[2048,768]{1,0:T(8,128)(2,1)}) %all-gather.16.cloned.1.call-update) | async-done | bytes 3145744 | tf_op jit(solution)/shard_map/while/body/eval_jaxpr/all_gather | solution.py:39
  674.7 11.5 convolution_convert_fusion
  686.2 196.8 %all-reduce.19.cloned.1.call-done = bf16[4,4,2,64,2048]{4,3,2,1,0:T(8,128)(2,1)} async-done(((bf16[4,4,2,64,2048]{4,3,2,1,0:T(8,128)(2,1)}), bf16[4,4,2,64,2048]{4,3,2,1,0:T(8,128)(2,1)}) %all-reduce.19.cloned.1.call-update) | async-done | bytes 8388624
  893.0 57.2 %all-gather.18.cloned.1.call-done = bf16[4,4,2,64,1024]{4,3,2,1,0:T(8,128)(2,1)} async-done(((bf16[4,4,1,64,1024]{4,3,2,1,0:T(8,128)(2,1)}), bf16[4,4,2,64,1024]{4,3,2,1,0:T(8,128)(2,1)}) %all-gather.18.cloned.1.call-update) | async-done | bytes 4194320 | tf_op jit(solution)/shard_map/while/body/eval_jaxpr/all_gather | solution.py:58
  958.9 59.0 %reduce-scatter.19.cloned.1.call-done = bf16[512,768]{1,0:T(8,128)(2,1)} async-done(((bf16[2048,768]{1,0:T(8,128)(2,1)}), bf16[512,768]{1,0:T(8,128)(2,1)}) %reduce-scatter.19.cloned.1.call-update) | async-done | bytes 786448 | tf_op jit(solution)/shard_map/while/body/eval_jaxpr/reduce_scatter | solution.py:43
  1020.5 63.6 %all-gather.20.cloned.1.call-done = bf16[2048,768]{1,0:T(8,128)(2,1)} async-done(((bf16[512,768]{1,0:T(8,128)(2,1)}), bf16[2048,768]{1,0:T(8,128)(2,1)}) %all-gather.20.cloned.1.call-update) | async-done | bytes 3145744 | tf_op jit(solution)/shard_map/while/body/eval_jaxpr/all_gather | solution.py:39
  1091.2 106.6 %all-reduce.21.cloned.1.call-done = bf16[4,4,2,64,1024]{4,3,2,1,0:T(8,128)(2,1)} async-done(((bf16[4,4,2,64,1024]{4,3,2,1,0:T(8,128)(2,1)}), bf16[4,4,2,64,1024]{4,3,2,1,0:T(8,128)(2,1)}) %all-reduce.21.cloned.1.call-update) | async-done | bytes 4194320
  1206.7 104.1 %all-gather.22.cloned.1.call-done = bf16[4,4,2,64,2048]{4,3,2,1,0:T(8,128)(2,1)} async-done(((bf16[4,4,1,64,2048]{4,3,2,1,0:T(8,128)(2,1)}), bf16[4,4,2,64,2048]{4,3,2,1,0:T(8,128)(2,1)}) %all-gather.22.cloned.1.call-update) | async-done | bytes 8388624 | tf_op jit(solution)/shard_map/while/body/eval_jaxpr/all_gather | solution.py:58
  1310.8 11.2 convolution_convert_fusion.3
  1322.2 60.4 %reduce-scatter.21.cloned.1.call-done = bf16[512,768]{1,0:T(8,128)(2,1)} async-done(((bf16[2048,768]{1,0:T(8,128)(2,1)}), bf16[512,768]{1,0:T(8,128)(2,1)}) %reduce-scatter.21.cloned.1.call-update) | async-done | bytes 786448 | tf_op jit(solution)/shard_map/while/body/eval_jaxpr/reduce_scatter | solution.py:43
  1393.9 7.9 convolution_convert_fusion.8
  1401.7 55.8 %all-gather.24.cloned.1.call-done = bf16[2048,768]{1,0:T(8,128)(2,1)} async-done(((bf16[512,768]{1,0:T(8,128)(2,1)}), bf16[2048,768]{1,0:T(8,128)(2,1)}) %all-gather.24.cloned.1.call-update) | async-done | bytes 3145744 | tf_op jit(solution)/shard_map/while/body/eval_jaxpr/all_gather | solution.py:39
  1462.4 12.4 convolution_convert_fusion.2
  1477.1 35.5 %all-reduce.23.cloned.1.call-done = bf16[4,4,2,64,384]{4,3,2,1,0:T(8,128)(2,1)} async-done(((bf16[4,4,2,64,384]{4,3,2,1,0:T(8,128)(2,1)}), bf16[4,4,2,64,384]{4,3,2,1,0:T(8,128)(2,1)}) %all-reduce.23.cloned.1.call-update) | async-done | bytes 1572880
  1529.1 9.4 multiply_reduce_fusion.1
  1538.5 8.0 convert_reduce_fusion.1
  1557.2 31.8 %convert_reduce_fusion.2 = (f32[8,6,64]{2,0,1:T(8,128)}, bf16[8,6,64,1152]{3,2,0,1:T(8,128)(2,1)}) fusion(f32[8,6,64,128]{3,2,0,1:T(8,128)S(1)} %copy-done.41, f32[8,6,64,1024]{3,2,0,1:T(8,128)} %bitcast.336, f32[8,6,64]{2,0,1:T(8,128)S(1)} %copy-done.57, f32[8,6,64,128]{3,2,0,1:T(8,128)S(1)} %copy-done.26, f32[8,6,64,1024]{3,2,0,1:T(8,128)} %copy-done.3), kind=kOutput, calls=%fused_computation.5 | output fusion | flops 42468480 | bytes 35414016 | tf_op jit(solution)/shard_map/while/body/eval_jaxpr/sub | solution.py:376
  1654.5 181.9 %all-reduce.26 = (bf16[4,512,768]{1,0,2:T(4,128)(2,1)}, f32[4,512,6]{1,0,2:T(4,128)S(1)}) all-reduce(f32[4,512,768]{1,0,2:T(4,128)} %pad_maximum_fusion.3, f32[4,512,6]{1,0,2:T(4,128)S(1)} %pad_maximum_fusion.12), channel_id=1, replica_groups=mesh['dp'=4,'row'=2,'col'=4] {'row'}, use_global_device_ids=true, to_apply=%region_29.30 | all-reduce | flops 1585152 | bytes 9535488 | tf_op jit(solution)/shard_map/while/body/eval_jaxpr/psum | solution.py:436
  1846.7 9.8 convolution_convert_fusion.4
  1866.0 23.3 %fusion.127 = f32[8,128,6]{2,0,1:T(8,128)S(1)} fusion(f32[8,128,6]{2,0,1:T(8,128)S(1)} %copy.286), kind=kOutput, calls=%fused_computation.243 | output fusion | flops 780288 | bytes 49152 | tf_op jit(solution)/shard_map/while/body/eval_jaxpr/reduce_window_sum | solution.py:443
  1902.8 41.2 %all-reduce.5 = (f32[]{:T(128)}, f32[]{:T(128)}) all-reduce(f32[]{:T(128)S(6)} %mul.379, f32[]{:T(128)S(6)} %mul.380), channel_id=1, replica_groups=mesh['dp'=4,'row'=2,'col'=4] {'dp','row','col'}, use_global_device_ids=true, to_apply=%region_19.20 | all-reduce | flops 2 | bytes 16 | tf_op jit(solution)/shard_map/psum | solution.py:541
  1948.8 11.2 all-reduce.8
  1961.2 40.5 %all-reduce.25.cloned.1.call-done = (bf16[768,1536]{1,0:T(8,128)(2,1)}, bf16[384,768]{1,0:T(8,128)(2,1)}, bf16[768,2048]{1,0:T(8,128)(2,1)}, bf16[1024,768]{1,0:T(8,128)(2,1)}) async-done(((bf16[768,1536]{1,0:T(8,128)(2,1)}, bf16[384,768]{1,0:T(8,128)(2,1)}, bf16[768,2048]{1,0:T(8,128)(2,1)}, bf16[1024,768]{1,0:T(8,128)(2,1)}), (bf16[768,1536]{1,0:T(8,128)(2,1)}, bf16[384,768]{1,0:T(8,128)(2,1)}, ...) | async-done | bytes 7667728 | tf_op jit(solution)/shard_map/psum | solution.py:533
  2014.0 50.3 %reduce-scatter.23.cloned.1.call-done = bf16[512,768]{1,0:T(8,128)(2,1)} async-done(((bf16[2048,768]{1,0:T(8,128)(2,1)}), bf16[512,768]{1,0:T(8,128)(2,1)}) %reduce-scatter.23.cloned.1.call-update) | async-done | bytes 786448 | tf_op jit(solution)/shard_map/while/body/eval_jaxpr/reduce_scatter | solution.py:43
  2066.1 33.1 %all-reduce.6 = (f32[768]{0:T(1024)S(1)}, f32[768]{0:T(1024)S(1)}) all-reduce(f32[768]{0:T(1024)S(1)} %get-tuple-element.85, f32[768]{0:T(1024)S(1)} %copy-done.75), channel_id=1, replica_groups=mesh['dp'=4,'row'=2,'col'=4] {'dp','col'}, use_global_device_ids=true, to_apply=%region_44.45 | all-reduce | flops 1536 | bytes 12288 | tf_op jit(solution)/shard_map/psum | solution.py:540
  (414 shorter events, 337.9 us)
Async XLA Ops:
  7.2 943.0 %copy-start = (bf16[1024,768]{1,0:T(8,128)(2,1)S(1)}, bf16[1024,768]{1,0:T(8,128)(2,1)}, u32[]{:S(2)}) copy-start(bf16[1024,768]{1,0:T(8,128)(2,1)} %param.39) | copy-start | bytes 4718596
  7.2 76.4 %all-gather.10.cloned.1.call-start = ((), (), s32[]{:S(2)}) async-start(), calls=%async_computation.4 | async-start | bytes 3932160 | tf_op jit(solution)/shard_map/while/body/eval_jaxpr/all_gather | solution.py:39
  18.2 362.3 %all-reduce.17.cloned.1.call-start = ((), (), s32[]{:S(2)}) async-start(), calls=%async_computation.17 | async-start | bytes 25165824
  93.6 347.7 %all-gather.12.cloned.1.call-start = ((), (), s32[]{:S(2)}) async-start(), calls=%async_computation.5 | async-start | bytes 4718592 | tf_op jit(solution)/shard_map/while/body/eval_jaxpr/all_gather | solution.py:214
  95.8 316.3 %copy-start.81 = (s32[8]{0:T(128)}, s32[8]{0:T(128)S(1)}, u32[]{:S(2)}) copy-start(s32[8]{0:T(128)S(1)} %broadcast_add_fusion) | copy-start | bytes 100
  387.3 148.3 %all-gather.14.cloned.1.call-start = ((), (), s32[]{:S(2)}) async-start(), calls=%async_computation.6 | async-start | bytes 2359296 | tf_op jit(solution)/shard_map/while/body/eval_jaxpr/all_gather | solution.py:58
  506.9 95.4 %reduce-scatter.17.cloned.1.call-start = ((), (), s32[]{:S(2)}) async-start(), calls=%async_computation.7 | async-start | bytes 3932160 | tf_op jit(solution)/shard_map/while/body/eval_jaxpr/reduce_scatter | solution.py:43
  541.8 60.4 %copy-start.6 = (bf16[1,2,128,768]{3,2,1,0:T(8,128)(2,1)S(1)}, bf16[1,2,128,768]{3,2,1,0:T(8,128)(2,1)}, u32[]{:S(2)}) copy-start(bf16[1,2,128,768]{3,2,1,0:T(8,128)(2,1)} %param.21) | copy-start | bytes 1179652
  541.8 60.4 %copy-start.8 = (bf16[1,256,768]{2,1,0:T(8,128)(2,1)S(1)}, bf16[1,256,768]{2,1,0:T(8,128)(2,1)}, u32[]{:S(2)}) copy-start(bf16[1,256,768]{2,1,0:T(8,128)(2,1)} %param.20) | copy-start | bytes 1179652
  541.8 132.9 %all-gather.16.cloned.1.call-start = ((), (), s32[]{:S(2)}) async-start(), calls=%async_computation.8 | async-start | bytes 3932160 | tf_op jit(solution)/shard_map/while/body/eval_jaxpr/all_gather | solution.py:39
  542.5 71.4 %copy-start.64 = (f32[768]{0:T(1024)}, f32[768]{0:T(1024)S(1)}, u32[]{:S(2)}) copy-start(f32[768]{0:T(1024)S(1)} %convert_element_type.261) | copy-start | bytes 9220
  611.0 272.0 %all-reduce.19.cloned.1.call-start = ((), (), s32[]{:S(2)}) async-start(), calls=%async_computation.18 | async-start | bytes 16777216
  686.2 264.0 %all-gather.18.cloned.1.call-start = ((), (), s32[]{:S(2)}) async-start(), calls=%async_computation.9 | async-start | bytes 6291456 | tf_op jit(solution)/shard_map/while/body/eval_jaxpr/all_gather | solution.py:58
  892.9 125.0 %reduce-scatter.19.cloned.1.call-start = ((), (), s32[]{:S(2)}) async-start(), calls=%async_computation.10 | async-start | bytes 3932160 | tf_op jit(solution)/shard_map/while/body/eval_jaxpr/reduce_scatter | solution.py:43
  957.5 60.4 %copy-start.12 = (bf16[512,768]{1,0:T(8,128)(2,1)S(1)}, bf16[512,768]{1,0:T(8,128)(2,1)}, u32[]{:S(2)}) copy-start(bf16[512,768]{1,0:T(8,128)(2,1)} %reduce-scatter.17.cloned.1.call-done) | copy-start | bytes 2359300
  957.5 60.4 %copy-start.27 = (bf16[1,2,128,768]{3,2,1,0:T(8,128)(2,1)S(1)}, bf16[1,2,128,768]{3,2,1,0:T(8,128)(2,1)}, u32[]{:S(2)}) copy-start(bf16[1,2,128,768]{3,2,1,0:T(8,128)(2,1)} %param.23) | copy-start | bytes 1179652
  957.5 126.7 %all-gather.20.cloned.1.call-start = ((), (), s32[]{:S(2)}) async-start(), calls=%async_computation.11 | async-start | bytes 3932160 | tf_op jit(solution)/shard_map/while/body/eval_jaxpr/all_gather | solution.py:39
  1020.5 177.3 %all-reduce.21.cloned.1.call-start = ((), (), s32[]{:S(2)}) async-start(), calls=%async_computation.19 | async-start | bytes 8388608
  1091.2 219.7 %all-gather.22.cloned.1.call-start = ((), (), s32[]{:S(2)}) async-start(), calls=%async_computation.12 | async-start | bytes 12582912 | tf_op jit(solution)/shard_map/while/body/eval_jaxpr/all_gather | solution.py:58
  1206.7 175.9 %reduce-scatter.21.cloned.1.call-start = ((), (), s32[]{:S(2)}) async-start(), calls=%async_computation.13 | async-start | bytes 3932160 | tf_op jit(solution)/shard_map/while/body/eval_jaxpr/reduce_scatter | solution.py:43
  1322.1 60.5 %copy-start.18 = (bf16[512,768]{1,0:T(8,128)(2,1)S(1)}, bf16[512,768]{1,0:T(8,128)(2,1)}, u32[]{:S(2)}) copy-start(bf16[512,768]{1,0:T(8,128)(2,1)} %reduce-scatter.19.cloned.1.call-done) | copy-start | bytes 2359300
  1322.1 60.5 %copy-start.28 = (bf16[1,256,768]{2,1,0:T(8,128)(2,1)S(1)}, bf16[1,256,768]{2,1,0:T(8,128)(2,1)}, u32[]{:S(2)}) copy-start(bf16[1,256,768]{2,1,0:T(8,128)(2,1)} %param.22) | copy-start | bytes 1179652
  1322.1 60.5 %copy-start.65 = (f32[768]{0:T(1024)S(1)}, f32[768]{0:T(1024)}, u32[]{:S(2)}) copy-start(f32[768]{0:T(1024)} %copy-done.64) | copy-start | bytes 9220
  1322.1 60.5 %copy-start.69 = (f32[512]{0:T(512)S(1)}, f32[512]{0:T(512)}, u32[]{:S(2)}) copy-start(f32[512]{0:T(512)} %add_convert_fusion.1) | copy-start | bytes 6148
  1322.1 60.5 %copy-start.73 = (f32[512]{0:T(512)S(1)}, f32[512]{0:T(512)}, u32[]{:S(2)}) copy-start(f32[512]{0:T(512)} %copy-done.72) | copy-start | bytes 6148
  1322.1 135.4 %all-gather.24.cloned.1.call-start = ((), (), s32[]{:S(2)}) async-start(), calls=%async_computation.14 | async-start | bytes 3932160 | tf_op jit(solution)/shard_map/while/body/eval_jaxpr/all_gather | solution.py:39
  1393.8 63.7 %copy-start.87 = (bf16[384,768]{1,0:T(8,128)(2,1)S(1)}, bf16[384,768]{1,0:T(8,128)(2,1)}, u32[]{:S(2)}) copy-start(bf16[384,768]{1,0:T(8,128)(2,1)} %param.35) | copy-start | bytes 1769476
  1393.8 118.8 %all-reduce.23.cloned.1.call-start = ((), (), s32[]{:S(2)}) async-start(), calls=%async_computation.20 | async-start | bytes 3145728
  1462.4 378.5 %all-gather.26.cloned.1.call-start = ((), (), s32[]{:S(2)}) async-start(), calls=%async_computation.15 | async-start | bytes 4718592 | tf_op jit(solution)/shard_map/while/body/eval_jaxpr/all_gather | solution.py:58
  1654.4 347.3 %all-reduce.25.cloned.1.call-start = ((), (), s32[]{:S(2)}) async-start(), calls=%async_computation.21 | async-start | bytes 15335424 | tf_op jit(solution)/shard_map/psum | solution.py:533
  1856.5 207.8 %reduce-scatter.23.cloned.1.call-start = ((), (), s32[]{:S(2)}) async-start(), calls=%async_computation.16 | async-start | bytes 3932160 | tf_op jit(solution)/shard_map/while/body/eval_jaxpr/reduce_scatter | solution.py:43
  2010.6 55.6 %copy-start.75 = (f32[768]{0:T(1024)S(1)}, f32[768]{0:T(1024)}, u32[]{:S(2)}) copy-start(f32[768]{0:T(1024)} %get-tuple-element.83) | copy-start | bytes 9220
  (78 other events, 793.5 us)
Sparse Core Ops, SparseCore 0:
  18.3 65.2 all-gather.9
  93.8 286.6 all-reduce.16
  387.4 46.5 all-gather.11
  507.0 28.5 all-gather.13
  542.0 60.2 reduce-scatter.16
  611.1 63.5 all-gather.15
  686.3 196.6 all-reduce.18
  893.0 57.0 all-gather.17
  957.6 60.2 reduce-scatter.18
  1020.6 63.5 all-gather.19
  1091.3 106.5 all-reduce.20
  1206.8 103.9 all-gather.21
  1322.2 60.2 reduce-scatter.20
  1393.9 63.5 all-gather.23
  1462.5 50.1 all-reduce.22
  1654.5 78.7 all-gather.25
  1856.6 144.9 all-reduce.24
  2003.9 60.3 reduce-scatter.22
where the time goes:
time: 2120 us
  waiting for transfers between devices  1320 us (62%)
  blocking collectives  303 us (14%)
  other arithmetic  194 us (9%)
  matrix products  171 us (8%)
  local copies, waits for them, and re-layouts  105 us (5%)
    unnamed x22, waiting for transfers between devices  624 us
    all_gather x4, waiting for transfers between devices, group_rows(): return lax.all_gather(local_rows, 'col', axis=0, tiled=True)  241 us
    reduce_scatter x4, waiting for transfers between devices, token_sums(): lax.psum_scatter(partial_rows.astype(jnp.bfloat16), 'col', scatter_dimens...  229 us
    all_gather x4, waiting for transfers between devices, head_rows(): gathered = lax.all_gather(own_rows, 'row', axis=2, tiled=True)  190 us
    psum x1, blocking collectives, one_group(): kv_grad_full, cum_grad_full = lax.psum((kv_grad_part, cum_grad_part), 'row')  182 us
  transfers between devices with their start and end apart: 18, of which 16 were waited for; matrix products, arithmetic and copies ran while one was open for 6% of the time, Pallas kernels for 0%

commit v1 on v0

--- a/solution.py
+++ b/solution.py
@@ -1,9 +1,15 @@
+import functools
+import itertools
+
 import jax
 import jax.numpy as jnp
 from jax import lax
-from jax.sharding import PartitionSpec as P
+from jax.experimental import pallas as pl
+from jax.experimental.pallas import tpu as pltpu
+from jax.sharding import Mesh, PartitionSpec as P
 
 D = 1536
+HEADS = 24
 HEAD_DIM = 64
 PROMPT = 1024
 CONTS = 8
@@ -98,7 +104,7 @@
     return jnp.concatenate([far_scores, near_scores], axis=-1)
 
 
-def body(
+def wide_body(
     x_prompt,
     x_cont,
     teacher_prompt,
@@ -562,44 +568,1585 @@
     )
 
 
-def solution(mesh):
+AX = ("yo", "y", "c", "x", "zh", "zl")
+FAR_PIECE = 18
+DOC_LANE = 36
+UNIT_LANE = 40
+NEVER = 1e12
+LANES = 128
+BF = jnp.bfloat16
+F32 = jnp.float32
+
+
+class Ring:
+    def __init__(self, sizes):
+        self.sizes = sizes
+        self.zl_count = sizes["zl"]
+        self.offsets = [(dy, dz) for dy in range(2) for dz in range(self.zl_count)]
+        self.back = [
+            self.offsets.index(((-dy) % 2, (-dz) % self.zl_count)) for dy, dz in self.offsets
+        ]
+
+    def pairs(self, target, source_ok=None):
+        ranges = [range(self.sizes[a]) for a in AX]
+        number = {}
+        for place, coords in enumerate(itertools.product(*ranges)):
+            number[coords] = place
+        out = []
+        for coords in number:
+            here = dict(zip(AX, coords))
+            if source_ok is not None and not source_ok(here):
+                continue
+            there = dict(here, **target(here))
+            out.append((number[coords], number[tuple(there[a] for a in AX)]))
+        return out
+
+    def move(self, value, target, source_ok=None):
+        return lax.ppermute(value, AX, self.pairs(target, source_ok))
+
+    def swap(self, value, axis, source_ok=None):
+        return self.move(value, lambda h: {axis: 1 - h[axis]}, source_ok)
+
+    def to_peer(self, value, k):
+        dy, dz = self.offsets[k]
+        return self.move(
+            value, lambda h: {"y": (h["y"] + dy) % 2, "zl": (h["zl"] + dz) % self.zl_count}
+        )
+
+    def to_group(self, value, flip):
+        return self.move(
+            value,
+            lambda h: {
+                "y": h["zh"],
+                "c": h["x"] ^ flip,
+                "x": h["y"],
+                "zh": h["c"],
+            },
+        )
+
+    def from_group(self, value, flip):
+        return self.move(
+            value,
+            lambda h: {"y": h["x"], "c": h["zh"], "x": h["c"] ^ flip, "zh": h["y"]},
+        )
+
+    def total(self, value):
+        for axis in ("c", "y", "x", "zh"):
+            value = value + self.swap(value, axis)
+        if self.zl_count == 2:
+            value = value + self.swap(value, "zl")
+        elif self.zl_count > 2:
+            value = lax.psum(value, "zl")
+        if self.sizes["yo"] > 1:
+            value = lax.psum(value, "yo")
+        return value
+
+    def gather(self, rows):
+        return [rows] + [self.to_peer(rows, k) for k in range(1, len(self.offsets))]
+
+    def scatter_sum(self, partial_of):
+        arrived = []
+        for k in range(1, len(self.offsets)):
+            arrived.append(self.to_peer(partial_of(self.back[k]).astype(BF), k))
+        total = partial_of(0)
+        for part in arrived:
+            total = total + part.astype(F32)
+        return total
+
+
+def nt_dot(left_op, right_op):
+    return lax.dot_general(
+        left_op, right_op, (((1,), (1,)), ((), ())), preferred_element_type=F32
+    )
+
+
+def tn_dot(left_op, right_op):
+    return lax.dot_general(
+        left_op, right_op, (((0,), (0,)), ((), ())), preferred_element_type=F32
+    )
+
+
+def nn_dot(left_op, right_op):
+    return jnp.dot(left_op, right_op, preferred_element_type=F32)
+
+
+def split_pieces(values, shift, heads):
+    high = values.astype(BF).astype(F32)
+    rest = values - high
+    mid = rest.astype(BF).astype(F32)
+    low = (rest - mid).astype(BF).astype(F32)
+    out = None
+    for place, piece in enumerate((high, mid, low)):
+        amount = shift + place * heads
+        moved = pltpu.roll(piece, amount, 1) if amount else piece
+        out = moved if out is None else out + moved
+    return out
+
+
+def head_lanes(shape, head, heads):
+    lane = lax.broadcasted_iota(jnp.int32, shape, len(shape) - 1)
+    keep = lane >= DOC_LANE
+    for place in range(3):
+        keep = keep | (lane == place * heads + head) | (lane == FAR_PIECE + place * heads + head)
+    return keep
+
+
+def half_lanes(shape, half):
+    lane = lax.broadcasted_iota(jnp.int32, shape, len(shape) - 1)
+    return (lane >= HEAD_DIM * half) & (lane < HEAD_DIM * (half + 1))
+
+
+def near_visible(rows):
+    key_row = lax.broadcasted_iota(jnp.int32, (rows, rows), 0)
+    query_row = lax.broadcasted_iota(jnp.int32, (rows, rows), 1)
+    same = (key_row // CLEN) == (query_row // CLEN)
+    return same & (key_row <= query_row)
+
+
+def fill_keys(
+    keys, flag, far_own, far_there, kv_near, cum_far, cum_near, far_base, near_base, far_rows, heads
+):
+    slots = heads // 2
+
+    @pl.when(pl.program_id(0) == 0)
+    def _():
+        aug = (far_base[...].astype(F32) + split_pieces(-cum_far[...], FAR_PIECE, heads)).astype(BF)
+        for s in range(slots):
+            keys[s, :far_rows, LANES:] = aug
+
+        @pl.when(flag[0] == 0)
+        def _():
+            for s in range(slots):
+                keys[s, :far_rows, :LANES] = far_own[s][:, :LANES]
+
+        @pl.when(flag[0] != 0)
+        def _():
+            for s in range(slots):
+                keys[s, :far_rows, :LANES] = far_there[s][:, :LANES]
+
+    aug = (near_base[...].astype(F32) + split_pieces(-cum_near[...], FAR_PIECE, heads)).astype(BF)
+    for s in range(slots):
+        keys[s, far_rows:, :LANES] = kv_near[s][:, :LANES]
+        keys[s, far_rows:, LANES:] = aug
+
+
+def attend_kernel(
+    heads,
+    flag,
+    qg_a,
+    qg_b,
+    qg_c,
+    near_a,
+    near_b,
+    near_c,
+    own_a,
+    own_b,
+    own_c,
+    there_a,
+    there_b,
+    there_c,
+    cum_near,
+    cum_far,
+    q_base,
+    near_base,
+    far_base,
+    gated_ref,
+    att_ref,
+    log_ref,
+    keys,
+    vals,
+):
+    qg = (qg_a, qg_b, qg_c)
+    kv_near = (near_a, near_b, near_c)
+    far_own = (own_a, own_b, own_c)
+    far_there = (there_a, there_b, there_c)
+    rows = qg_a.shape[0]
+    far_rows = own_a.shape[0]
+    slots = heads // 2
+    fill_keys(
+        keys,
+        flag,
+        far_own,
+        far_there,
+        kv_near,
+        cum_far,
+        cum_near,
+        far_base,
+        near_base,
+        far_rows,
+        heads,
+    )
+
+    @pl.when(pl.program_id(0) == 0)
+    def _():
+        def fill(source):
+            for s in range(slots):
+                moved = source[s][:, LANES:].T
+                for half in range(2):
+                    vals[2 * s + half, :HEAD_DIM, :far_rows] = moved[
+                        HEAD_DIM * half : HEAD_DIM * (half + 1)
+                    ]
+
+        @pl.when(flag[0] == 0)
+        def _():
+            fill(far_own)
+
+        @pl.when(flag[0] != 0)
+        def _():
+            fill(far_there)
+
+        for h in range(heads):
+            vals[h, HEAD_DIM:, :] = jnp.ones((16, far_rows + rows), BF)
+
+    for s in range(slots):
+        moved = kv_near[s][:, LANES:].T
+        for half in range(2):
+            vals[2 * s + half, :HEAD_DIM, far_rows:] = moved[
+                HEAD_DIM * half : HEAD_DIM * (half + 1)
+            ]
+    q_aug = (q_base[...].astype(F32) + split_pieces(cum_near[...], 0, heads)).astype(BF)
+    visible = near_visible(rows)
+    outs = []
+    logs = []
+    for h in range(heads):
+        s, half = h // 2, h % 2
+        query = qg[s][:, :LANES]
+        query = jnp.where(half_lanes(query.shape, half), query * BF(HEAD_DIM**-0.5), BF(0))
+        aug = jnp.where(head_lanes(q_aug.shape, h, heads), q_aug, BF(0))
+        q_cat = jnp.concatenate([query, aug], axis=1)
+        far = nt_dot(keys[s, :far_rows], q_cat)
+        near = jnp.where(visible, nt_dot(keys[s, far_rows:], q_cat), -NEVER)
+        top = jnp.maximum(
+            jnp.max(far, axis=0, keepdims=True), jnp.max(near, axis=0, keepdims=True)
+        )
+        far_p = jnp.exp(far - top).astype(BF)
+        near_p = jnp.exp(near - top).astype(BF)
+        out = nn_dot(vals[h, :, :far_rows], far_p) + nn_dot(vals[h, :, far_rows:], near_p)
+        total = out[HEAD_DIM : HEAD_DIM + 1]
+        outs.append(out[:HEAD_DIM] / total)
+        logs.append(top + jnp.log(total))
+    att = jnp.concatenate(outs, axis=0).T
+    att_ref[...] = att
+    for s in range(slots):
+        gate = qg[s][:, LANES:].astype(F32)
+        cols = slice(s * LANES, (s + 1) * LANES)
+        gated_ref[:, cols] = (att[:, cols] * jax.nn.sigmoid(gate)).astype(BF)
+    log_rows = jnp.concatenate(logs + [jnp.zeros((LANES - heads, rows), F32)], axis=0)
+    log_ref[...] = log_rows.T
+
+
+def row_block(rows, cols, place=0):
+    return pl.BlockSpec((rows, cols), lambda i: (i, place))
+
+
+def whole_block(rows, cols):
+    return pl.BlockSpec((rows, cols), lambda i: (0, 0))
+
+
+def slot_inputs(flag, projects, kv_there, rows):
+    far_rows = projects[0].shape[0]
+    specs_in = [pl.BlockSpec(memory_space=pltpu.SMEM)]
+    for spec in (
+        row_block(rows, 2 * LANES),
+        row_block(rows, 2 * LANES, 1),
+        pl.BlockSpec((far_rows, 2 * LANES), lambda i: (0, 1)),
+        whole_block(far_rows, 2 * LANES),
+    ):
+        specs_in += [spec] * len(projects)
+    return specs_in, [flag, *projects, *projects, *projects, *kv_there]
+
+
+def cum_specs(rows, far_rows):
+    return [
+        row_block(rows, LANES),
+        whole_block(far_rows, LANES),
+        row_block(rows, LANES),
+        row_block(rows, LANES),
+        whole_block(far_rows, LANES),
+    ]
+
+
+def attend(flag, projects, kv_there, cum_near, cum_far, q_base, near_base, far_base, rows, heads):
+    total = projects[0].shape[0]
+    width = heads * HEAD_DIM
+    steps = total // rows
+    flops = 2 * total * (total + rows) * heads * 384
+    slot_specs, slot_values = slot_inputs(flag, projects, kv_there, rows)
+    return pl.pallas_call(
+        functools.partial(attend_kernel, heads),
+        grid=(steps,),
+        out_shape=(
+            jax.ShapeDtypeStruct((total, width), BF),
+            jax.ShapeDtypeStruct((total, width), F32),
+            jax.ShapeDtypeStruct((total, LANES), F32),
+        ),
+        in_specs=slot_specs + cum_specs(rows, total),
+        out_specs=(row_block(rows, width), row_block(rows, width), row_block(rows, LANES)),
+        scratch_shapes=[
+            pltpu.VMEM((heads // 2, total + rows, 2 * LANES), BF),
+            pltpu.VMEM((heads, HEAD_DIM + 16, total + rows), BF),
+        ],
+        compiler_params=pltpu.CompilerParams(vmem_limit_bytes=48 << 20),
+        cost_estimate=pl.CostEstimate(
+            flops=flops, bytes_accessed=total * width * 20, transcendentals=total * total * heads
+        ),
+    )(*slot_values, cum_near, cum_far, q_base, near_base, far_base)
+
+
+def attend_back_kernel(
+    heads,
+    flag,
+    qg_a,
+    qg_b,
+    qg_c,
+    near_a,
+    near_b,
+    near_c,
+    own_a,
+    own_b,
+    own_c,
+    there_a,
+    there_b,
+    there_c,
+    cum_near,
+    cum_far,
+    q_base,
+    near_base,
+    far_base,
+    grad_ref,
+    att_ref,
+    log_ref,
+    dqg_ref,
+    near_ref,
+    far_ref,
+    row_ref,
+    near_col,
+    far_col,
+    keys,
+    vals,
+):
+    qg = (qg_a, qg_b, qg_c)
+    kv_near = (near_a, near_b, near_c)
+    far_own = (own_a, own_b, own_c)
+    far_there = (there_a, there_b, there_c)
+    rows = qg_a.shape[0]
+    far_rows = own_a.shape[0]
+    slots = heads // 2
+    fill_keys(
+        keys,
+        flag,
+        far_own,
+        far_there,
+        kv_near,
+        cum_far,
+        cum_near,
+        far_base,
+        near_base,
+        far_rows,
+        heads,
+    )
+
+    @pl.when(pl.program_id(0) == 0)
+    def _():
+        lane = lax.broadcasted_iota(jnp.int32, (far_rows + rows, LANES), 1)
+        ones = (lane < 3).astype(F32).astype(BF)
+        for s in range(slots):
+            vals[s, :, LANES:] = ones
+
+        @pl.when(flag[0] == 0)
+        def _():
+            for s in range(slots):
+                vals[s, :far_rows, :LANES] = far_own[s][:, LANES:]
+
+        @pl.when(flag[0] != 0)
+        def _():
+            for s in range(slots):
+                vals[s, :far_rows, :LANES] = far_there[s][:, LANES:]
+
+        far_ref[...] = jnp.zeros(far_ref.shape, F32)
+        far_col[...] = jnp.zeros(far_col.shape, F32)
+
+    for s in range(slots):
+        vals[s, far_rows:, :LANES] = kv_near[s][:, LANES:]
+    q_aug = (q_base[...].astype(F32) + split_pieces(cum_near[...] - log_ref[...], 0, heads)).astype(
+        BF
+    )
+    visible = near_visible(rows)
+    lane = lax.broadcasted_iota(jnp.int32, (rows, LANES), 1)
+    row_total = jnp.zeros((rows, LANES), F32)
+    col_total = jnp.zeros((rows, LANES), F32)
+    for s in range(slots):
+        cols = slice(s * LANES, (s + 1) * LANES)
+        kcols = slice(2 * s * LANES, (2 * s + 1) * LANES)
+        vcols = slice((2 * s + 1) * LANES, (2 * s + 2) * LANES)
+        gate_sig = jax.nn.sigmoid(qg[s][:, LANES:].astype(F32))
+        grad = grad_ref[:, cols].astype(F32)
+        att = att_ref[:, cols]
+        grad_att = (grad * gate_sig).astype(BF)
+        dqg_ref[:, vcols] = (grad * att * gate_sig * (1.0 - gate_sig)).astype(BF)
+        weighed = grad_att.astype(F32) * att
+        dq_total = jnp.zeros((rows, LANES), F32)
+        dk_near = jnp.zeros((rows, LANES), F32)
+        dv_near = jnp.zeros((rows, LANES), F32)
+        for half in range(2):
+            h = 2 * s + half
+            mine = half_lanes((rows, LANES), half)
+            query = jnp.where(mine, qg[s][:, :LANES] * BF(HEAD_DIM**-0.5), BF(0))
+            aug = jnp.where(head_lanes(q_aug.shape, h, heads), q_aug, BF(0))
+            q_cat = jnp.concatenate([query, aug], axis=1)
+            ga = jnp.where(mine, grad_att, BF(0))
+            delta = -jnp.sum(jnp.where(mine, weighed, 0.0), axis=1, keepdims=True)
+            high = delta.astype(BF).astype(F32)
+            mid = (delta - high).astype(BF).astype(F32)
+            low = delta - high - mid
+            d_aug = jnp.where(
+                lane == 0, high, jnp.where(lane == 1, mid, jnp.where(lane == 2, low, 0.0))
+            ).astype(BF)
+            ga_cat = jnp.concatenate([ga, d_aug], axis=1)
+            for part in range(2):
+                span = slice(0, far_rows) if part == 0 else slice(far_rows, far_rows + rows)
+                prob = jnp.exp(nt_dot(keys[s, span], q_cat))
+                if part == 1:
+                    prob = jnp.where(visible, prob, 0.0)
+                ds = (prob * nt_dot(vals[s, span], ga_cat)).astype(BF)
+                dv = nn_dot(prob.astype(BF), ga)
+                dk = nn_dot(ds, q_cat)
+                dq = tn_dot(ds, keys[s, span])
+                dq_total += jnp.where(mine, dq[:, :LANES], 0.0)
+                row_total += jnp.where(lane == h, dq[:, LANES:], 0.0)
+                if part == 0:
+                    far_ref[:, kcols] += dk[:, :LANES]
+                    far_ref[:, vcols] += dv
+                    far_col[...] += dk[:, LANES:]
+                else:
+                    dk_near += dk[:, :LANES]
+                    dv_near += dv
+                    col_total += dk[:, LANES:]
+        dqg_ref[:, kcols] = (dq_total * HEAD_DIM**-0.5).astype(BF)
+        near_ref[:, kcols] = dk_near
+        near_ref[:, vcols] = dv_near
+    row_ref[...] = row_total
+    near_col[...] = col_total
+
+
+def attend_back(
+    flag,
+    projects,
+    kv_there,
+    cum_near,
+    cum_far,
+    q_base,
+    near_base,
+    far_base,
+    grad,
+    att,
+    logs,
+    rows,
+    heads,
+):
+    total = projects[0].shape[0]
+    width = heads * HEAD_DIM
+    steps = total // rows
+    flops = 2 * total * (total + rows) * heads * 1152
+    slot_specs, slot_values = slot_inputs(flag, projects, kv_there, rows)
+    return pl.pallas_call(
+        functools.partial(attend_back_kernel, heads),
+        grid=(steps,),
+        out_shape=(
+            jax.ShapeDtypeStruct((total, 2 * width), BF),
+            jax.ShapeDtypeStruct((total, 2 * width), F32),
+            jax.ShapeDtypeStruct((total, 2 * width), F32),
+            jax.ShapeDtypeStruct((total, LANES), F32),
+            jax.ShapeDtypeStruct((total, LANES), F32),
+            jax.ShapeDtypeStruct((total, LANES), F32),
+        ),
+        in_specs=slot_specs
+        + cum_specs(rows, total)
+        + [row_block(rows, width), row_block(rows, width), row_block(rows, LANES)],
+        out_specs=(
+            row_block(rows, 2 * width),
+            row_block(rows, 2 * width),
+            whole_block(total, 2 * width),
+            row_block(rows, LANES),
+            row_block(rows, LANES),
+            whole_block(total, LANES),
+        ),
+        scratch_shapes=[
+            pltpu.VMEM((heads // 2, total + rows, 2 * LANES), BF),
+            pltpu.VMEM((heads // 2, total + rows, 2 * LANES), BF),
+        ],
+        compiler_params=pltpu.CompilerParams(vmem_limit_bytes=56 << 20),
+        cost_estimate=pl.CostEstimate(
+            flops=flops, bytes_accessed=total * width * 40, transcendentals=total * total * heads
+        ),
+    )(*slot_values, cum_near, cum_far, q_base, near_base, far_base, grad, att, logs)
+
+
+def full_norm(tokens, gain_vec):
+    factor = lax.rsqrt(jnp.mean(tokens * tokens, axis=-1, keepdims=True) + epsilon)
+    scaled = tokens * factor
+    return factor, scaled, (scaled * gain_vec).astype(BF)
+
+
+def full_norm_back(grad_normed, factor, scaled, gain_vec):
+    e = grad_normed * gain_vec
+    mean = jnp.mean(e * scaled, axis=-1, keepdims=True)
+    return jnp.sum(grad_normed * scaled, axis=0), factor * (e - scaled * mean)
+
+
+MESH_ID = pl.DeviceIdType.MESH
+
+
+class Here:
+    def __init__(self, ring):
+        self.ring = ring
+        self.at = {a: lax.axis_index(a) for a in AX}
+
+    def other(self, axis):
+        return {axis: 1 - self.at[axis]}
+
+    def peer(self, k):
+        dy, dz = self.ring.offsets[k]
+        return {
+            "y": lax.rem(self.at["y"] + dy, 2),
+            "zl": lax.rem(self.at["zl"] + dz, self.ring.zl_count),
+        }
+
+    def greet(self, targets, extra=()):
+        barrier = pltpu.get_barrier_semaphore()
+        for target in targets:
+            pl.semaphore_signal(barrier, inc=1, device_id=target, device_id_type=MESH_ID)
+        count = len(targets)
+        for target, away in extra:
+            @pl.when(away)
+            def _():
+                pl.semaphore_signal(barrier, inc=1, device_id=target, device_id_type=MESH_ID)
+
+            count = count + away.astype(jnp.int32)
+        pl.semaphore_wait(barrier, count)
+
+
+def remote(src, dst, send_sem, recv_sem, target):
+    return pltpu.make_async_remote_copy(
+        src_ref=src,
+        dst_ref=dst,
+        send_sem=send_sem,
+        recv_sem=recv_sem,
+        device_id=target,
+        device_id_type=MESH_ID,
+    )
+
+
+def last_kernel(
+    ring,
+    grads_in,
+    weight_in,
+    normed_in,
+    tokens_in,
+    residual_in,
+    gain_in,
+    hid_in,
+    down_in,
+    out_first_in,
+    out_mid_in,
+    back_out,
+    proj_out,
+    gate_out,
+    up_out,
+    down_out,
+    out_out,
+    gain_out,
+    grads,
+    weight,
+    normed,
+    tokens,
+    residual,
+    rs_send,
+    rs_land,
+    total,
+    c_send,
+    c_land,
+    kept,
+    x_send,
+    x_land,
+    z_send,
+    z_land,
+    final,
+    blocks,
+    gain_sum,
+    gain_nat,
+    gain_land,
+    load_sem,
+    local_sem,
+    y_send_sem,
+    y_recv_sem,
+    c2_send_sem,
+    c2_recv_sem,
+    rs_send_sem,
+    rs_recv_sem,
+    c_send_sem,
+    c_recv_sem,
+    x_send_sem,
+    x_recv_sem,
+    z_send_sem,
+    z_recv_sem,
+    back_send_sem,
+    back_recv_sem,
+    gain_send_sem,
+    gain_recv_sem,
+):
+    here = Here(ring)
+    y, c, x, zh = (here.at[a] for a in ("y", "c", "x", "zh"))
+    local, features = tokens.shape
+    part = features // 4
+    slot_w = 4 * LANES
+    slots = z_count = 3
+    units = down_in.shape[0]
+    owner = zh == y
+    peers = len(ring.offsets)
+
+    loads = [
+        pltpu.make_async_copy(a, b, load_sem.at[i])
+        for i, (a, b) in enumerate(
+            (
+                (grads_in, grads),
+                (weight_in, weight),
+                (normed_in, normed),
+                (tokens_in, tokens),
+                (residual_in, residual),
+            )
+        )
+    ]
+    for copy in loads:
+        copy.start()
+
+    def back_target(flip):
+        return {"y": x, "c": zh, "x": c ^ flip, "zh": y}
+
+    def back_away(flip):
+        return ~((x == y) & (zh == c) & ((c ^ flip) == x) & (zh == y))
+
+    def back_from_away(flip):
+        return ~((zh == y) & ((x ^ flip) == c) & (y == x) & (c == zh))
+
+    here.greet(
+        [here.peer(k) for k in range(1, peers)]
+        + [here.other("c"), here.other("x"), here.other("zh")],
+        [(back_target(f), back_away(f)) for f in range(2)]
+        + [({"y": zh, "c": x ^ f, "x": y, "zh": c}, back_from_away(f)) for f in range(2)],
+    )
+
+    row0 = pl.multiple_of(c * part, part)
+
+    def rows_of(ref, col, width):
+        return ref.at[pl.ds(row0, part), pl.ds(pl.multiple_of(col, LANES), width)]
+
+    def cols_of(ref, row, height):
+        return ref.at[pl.ds(pl.multiple_of(row, LANES), height), pl.ds(row0, part)]
+
+    pieces = [
+        (hid_in.at[:, :units], rows_of(gate_out, y * units, units)),
+        (hid_in.at[:, units:], rows_of(up_out, y * units, units)),
+        (down_in, cols_of(down_out, y * units, units)),
+        (out_first_in, cols_of(out_out, 2 * LANES * y, LANES)),
+    ]
+    own_pieces = [
+        pltpu.make_async_copy(src, dst, local_sem.at[i]) for i, (src, dst) in enumerate(pieces)
+    ]
+    y_pieces = [
+        remote(src, dst, y_send_sem.at[i], y_recv_sem.at[i], here.other("y"))
+        for i, (src, dst) in enumerate(pieces)
+    ]
+    mid_dst = cols_of(out_out, LANES, LANES)
+    own_mid = pltpu.make_async_copy(out_mid_in, mid_dst, local_sem.at[4])
+    y_mid = remote(out_mid_in, mid_dst, y_send_sem.at[4], y_recv_sem.at[4], here.other("y"))
+
+    loads[0].wait()
+    loads[1].wait()
+    tiles = 3
+    tile_w = features // tiles
+
+    def partial_rows(chunk_no, store):
+        def step(i, carry):
+            cols = pl.ds(pl.multiple_of(i * tile_w, LANES), tile_w)
+            store(
+                cols,
+                nt_dot(grads[chunk_no * local : (chunk_no + 1) * local, :], weight[cols, :]),
+            )
+            return carry
+
+        lax.fori_loop(0, tiles, step, 0)
+
+    rs = []
+    for k in range(1, peers):
+
+        def store_out(cols, value, k=k):
+            rs_send[k - 1, :, cols] = value.astype(BF)
+
+        partial_rows(ring.back[k], store_out)
+        copy = remote(
+            rs_send.at[k - 1],
+            rs_land.at[k - 1],
+            rs_send_sem.at[k - 1],
+            rs_recv_sem.at[k - 1],
+            here.peer(k),
+        )
+        copy.start()
+        rs.append(copy)
+    for copy in own_pieces + y_pieces:
+        copy.start()
+
+    @pl.when(owner)
+    def _():
+        own_mid.start()
+        y_mid.start()
+
+    loads[2].wait()
+    tile_r = LANES
+    per_part = part // tile_r
+
+    def weight_tile(first, i):
+        cols = pl.ds(pl.multiple_of(first + i * tile_r, LANES), tile_r)
+        return tn_dot(normed[:, cols], grads[:, : slots * slot_w])
+
+    def c_step(i, carry):
+        rows = pl.ds(pl.multiple_of(i * tile_r, tile_r), tile_r)
+        c_send[rows, :] = weight_tile(2 * part, i).astype(BF)
+        return carry
+
+    lax.fori_loop(0, 2 * per_part, c_step, 0)
+    c_copy = remote(c_send, c_land, c_send_sem, c_recv_sem, here.other("c"))
+    c_copy.start()
+
+    def store_own(cols, value):
+        total[:, cols] = value
+
+    partial_rows(0, store_own)
+    c_copy.wait_recv()
+
+    def x_step(i, carry):
+        rows = pl.ds(pl.multiple_of(i * tile_r, tile_r), tile_r)
+        land = pl.ds(pl.multiple_of(part + i * tile_r, tile_r), tile_r)
+        value = weight_tile(part, i) + c_land[land, :].astype(F32)
+        for s in range(slots):
+            x_send[s, rows, :] = value[:, s * slot_w : (s + 1) * slot_w].astype(BF)
+        return carry
+
+    lax.fori_loop(0, per_part, x_step, 0)
+    x_copies = {}
+    for s in (2, 1, 0):
+        x_copies[s] = remote(
+            x_send.at[s], x_land.at[s], x_send_sem.at[s], x_recv_sem.at[s], here.other("x")
+        )
+        x_copies[s].start()
+
+    def own_step(i, carry):
+        rows = pl.ds(pl.multiple_of(i * tile_r, tile_r), tile_r)
+        value = weight_tile(0, i) + c_land[rows, :].astype(F32)
+        for s in range(slots):
+            kept[s, rows, :] = value[:, s * slot_w : (s + 1) * slot_w]
+        return carry
+
+    lax.fori_loop(0, per_part, own_step, 0)
+
+    loads[3].wait()
+    loads[4].wait()
+    for copy in rs:
+        copy.wait_recv()
+    gain_sum[...] = jnp.zeros(gain_sum.shape, F32)
+    tile_n = 32
+
+    def norm_step(i, carry):
+        rows = pl.ds(pl.multiple_of(i * tile_n, tile_n), tile_n)
+        tok = tokens[rows, :].astype(F32)
+        grad = total[rows, :]
+        for k in range(peers - 1):
+            grad = grad + rs_land[k, rows, :].astype(F32)
+        factor = lax.rsqrt(jnp.mean(tok * tok, axis=-1, keepdims=True) + epsilon)
+        scaled_tok = tok * factor
+        e = grad * gain_in[...]
+        mean = jnp.mean(e * scaled_tok, axis=-1, keepdims=True)
+        out = factor * (e - scaled_tok * mean) + residual[rows, :]
+        weighed = jnp.sum(grad * scaled_tok, axis=0, keepdims=True)
+        for i in range(4):
+            blocks[i, rows, :] = out[:, i * part : (i + 1) * part].astype(BF)
+            gain_sum[i, 0:1, :] += weighed[:, i * part : (i + 1) * part]
+        return carry
+
+    lax.fori_loop(0, local // tile_n, norm_step, 0)
+
+    def block_no(half, low_high):
+        return (half ^ x) + 2 * (low_high ^ c)
+
+    def back_copy(flip, p):
+        return remote(
+            blocks.at[block_no(c ^ flip, p)],
+            back_out.at[c, :, p * part : (p + 1) * part],
+            back_send_sem.at[flip, p],
+            back_recv_sem.at[flip, p],
+            back_target(flip),
+        )
+
+    def back_own(flip, p):
+        return pltpu.make_async_copy(
+            blocks.at[block_no(c ^ flip, p)],
+            back_out.at[c, :, p * part : (p + 1) * part],
+            local_sem.at[5 + p],
+        )
+
+    for f in range(2):
+
+        @pl.when(back_away(f))
+        def _():
+            for p in range(2):
+                back_copy(f, p).start()
+
+        @pl.when(~back_away(f))
+        def _():
+            for p in range(2):
+                back_own(f, p).start()
+
+    z_copies = {}
+    for s in (2, 1, 0):
+        x_copies[s].wait_recv()
+        kept[s] += x_land[s].astype(F32)
+        if s == 2:
+            z_send[0] = kept[2].astype(BF)
+            z_copies[0] = remote(
+                z_send.at[0], z_land.at[0], z_send_sem.at[0], z_recv_sem.at[0], here.other("zh")
+            )
+            z_copies[0].start()
+        if s == 1:
+            z_copies[1] = remote(
+                z_send.at[1], z_land.at[1], z_send_sem.at[1], z_recv_sem.at[1], here.other("zh")
+            )
+
+            @pl.when(~owner)
+            def _():
+                z_send[1] = kept[1].astype(BF)
+                z_copies[1].start()
+
+    for copy in own_pieces:
+        copy.wait()
+    for copy in y_pieces:
+        copy.wait_recv()
+
+    @pl.when(owner)
+    def _():
+        own_mid.wait()
+
+    @pl.when(~owner)
+    def _():
+        y_mid.wait_recv()
+
+    c2 = []
+    for i, view in enumerate(
+        (
+            gate_out.at[pl.ds(row0, part), :],
+            up_out.at[pl.ds(row0, part), :],
+            down_out.at[:, pl.ds(row0, part)],
+            out_out.at[:, pl.ds(row0, part)],
+        )
+    ):
+        copy = remote(view, view, c2_send_sem.at[i], c2_recv_sem.at[i], here.other("c"))
+        copy.start()
+        c2.append(copy)
+
+    for i in range(4):
+        gain_nat[0, i] = gain_sum[block_no(i // 2, i % 2)]
+    for place, axis in enumerate(("c", "y", "x", "zl", "zh")):
+        copy = remote(
+            gain_nat.at[place],
+            gain_land.at[place],
+            gain_send_sem.at[place],
+            gain_recv_sem.at[place],
+            here.other(axis),
+        )
+        copy.start()
+        copy.wait_recv()
+        gain_nat[place + 1] = gain_nat[place] + gain_land[place]
+        copy.wait_send()
+    gain_copy = pltpu.make_async_copy(gain_nat.at[5], gain_out, local_sem.at[7])
+    gain_copy.start()
+
+    z_copies[0].wait_recv()
+    final[0] = (kept[0] + z_land[0].astype(F32)).astype(BF)
+
+    @pl.when(owner)
+    def _():
+        z_copies[1].wait_recv()
+        final[1] = (kept[1] + z_land[1].astype(F32)).astype(BF)
+
+    first_dst = rows_of(proj_out, 2 * y * slot_w, slot_w)
+    mid_proj = rows_of(proj_out, slot_w, slot_w)
+    own_first = pltpu.make_async_copy(final.at[0], first_dst, local_sem.at[8])
+    own_second = pltpu.make_async_copy(final.at[1], mid_proj, local_sem.at[9])
+    y_first = remote(final.at[0], first_dst, y_send_sem.at[5], y_recv_sem.at[5], here.other("y"))
+    y_second = remote(final.at[1], mid_proj, y_send_sem.at[6], y_recv_sem.at[6], here.other("y"))
+    y_first.start()
+    own_first.start()
+
+    @pl.when(owner)
+    def _():
+        y_second.start()
+        own_second.start()
+
+    own_first.wait()
+    y_first.wait_recv()
+
+    @pl.when(owner)
+    def _():
+        own_second.wait()
+
+    @pl.when(~owner)
+    def _():
+        y_second.wait_recv()
+
+    view = proj_out.at[pl.ds(row0, part), :]
+    copy = remote(view, view, c2_send_sem.at[4], c2_recv_sem.at[4], here.other("c"))
+    copy.start()
+    c2.append(copy)
+
+    for copy in c2:
+        copy.wait()
+    for f in range(2):
+
+        @pl.when(back_away(f))
+        def _():
+            for p in range(2):
+                back_copy(f, p).wait()
+
+        @pl.when(~back_away(f))
+        def _():
+            for p in range(2):
+                back_own(f, p).wait()
+
+    gain_copy.wait()
+    for copy in rs + [c_copy, x_copies[0], x_copies[1], x_copies[2], z_copies[0], y_first]:
+        copy.wait_send()
+    for copy in y_pieces:
+        copy.wait_send()
+
+    @pl.when(owner)
+    def _():
+        y_mid.wait_send()
+        y_second.wait_send()
+
+    @pl.when(~owner)
+    def _():
+        z_copies[1].wait_send()
+
+
+def last_step(ring, grads, weight, normed, tokens, residual, gain, hid, down, out_first, out_mid):
+    local, features = tokens.shape
+    rows = grads.shape[0]
+    part = features // 4
+    half = features // 2
+    units = down.shape[0]
+    peers = len(ring.offsets)
+    slot_w = 4 * LANES
+    any_spec = pl.BlockSpec(memory_space=pl.ANY)
+    dma = pltpu.SemaphoreType.DMA
+    return pl.pallas_call(
+        functools.partial(last_kernel, ring),
+        out_shape=(
+            jax.ShapeDtypeStruct((2, local, half), BF),
+            jax.ShapeDtypeStruct((half, 3 * slot_w), BF),
+            jax.ShapeDtypeStruct((half, 2 * units), BF),
+            jax.ShapeDtypeStruct((half, 2 * units), BF),
+            jax.ShapeDtypeStruct((2 * units, half), BF),
+            jax.ShapeDtypeStruct((3 * LANES, half), BF),
+            jax.ShapeDtypeStruct((4, 8, part), F32),
+        ),
+        in_specs=[any_spec] * 5 + [pl.BlockSpec(memory_space=pltpu.VMEM)] + [any_spec] * 4,
+        out_specs=[any_spec] * 7,
+        scratch_shapes=[
+            pltpu.VMEM(grads.shape, BF),
+            pltpu.VMEM(weight.shape, BF),
+            pltpu.VMEM(normed.shape, BF),
+            pltpu.VMEM(tokens.shape, BF),
+            pltpu.VMEM(residual.shape, F32),
+            pltpu.VMEM((peers - 1, local, features), BF),
+            pltpu.VMEM((peers - 1, local, features), BF),
+            pltpu.VMEM((local, features), F32),
+            pltpu.VMEM((half, 3 * slot_w), BF),
+            pltpu.VMEM((half, 3 * slot_w), BF),
+            pltpu.VMEM((3, part, slot_w), F32),
+            pltpu.VMEM((3, part, slot_w), BF),
+            pltpu.VMEM((3, part, slot_w), BF),
+            pltpu.VMEM((2, part, slot_w), BF),
+            pltpu.VMEM((2, part, slot_w), BF),
+            pltpu.VMEM((2, part, slot_w), BF),
+            pltpu.VMEM((4, local, part), BF),
+            pltpu.VMEM((4, 8, part), F32),
+            pltpu.VMEM((6, 4, 8, part), F32),
+            pltpu.VMEM((5, 4, 8, part), F32),
+            dma((5,)),
+            dma((10,)),
+            dma((7,)),
+            dma((7,)),
+            dma((5,)),
+            dma((5,)),
+            dma((peers - 1,)),
+            dma((peers - 1,)),
+            dma,
+            dma,
+            dma((3,)),
+            dma((3,)),
+            dma((2,)),
+            dma((2,)),
+            dma((2, 2)),
+            dma((2, 2)),
+            dma((5,)),
+            dma((5,)),
+        ],
+        compiler_params=pltpu.CompilerParams(
+            collective_id=1, has_side_effects=True, vmem_limit_bytes=58 << 20
+        ),
+        cost_estimate=pl.CostEstimate(
+            flops=4 * rows * features * 3 * slot_w, bytes_accessed=40 << 20, transcendentals=0
+        ),
+    )(grads, weight, normed, tokens, residual, gain, hid, down, out_first, out_mid)
+
+
+def ring_body(
+    ring,
+    x_prompt,
+    x_cont,
+    teacher_prompt,
+    teacher_cont,
+    segment_ids,
+    offsets,
+    prompt_valid,
+    cont_valid,
+    first_gain,
+    w_query,
+    w_key,
+    w_value,
+    w_outgate,
+    w_forget,
+    forget_bias,
+    w_out,
+    second_gain,
+    w_gate,
+    w_up,
+    w_down,
+):
+    y = lax.axis_index("y")
+    c = lax.axis_index("c")
+    x = lax.axis_index("x")
+    zh = lax.axis_index("zh")
+    zl = lax.axis_index("zl")
+    zl_count = ring.zl_count
+    local = x_prompt.shape[1]
+    half_d = x_prompt.shape[2]
+    part_d = half_d // 2
+    local_conts = x_cont.shape[1]
+    heads = w_forget.shape[1]
+    units_here = w_gate.shape[1]
+    half_units = units_here // 2
+    width = heads * HEAD_DIM
+    slots = heads // 2
+    pair_unit = PROMPT // CLEN
+    chunk_units = local // CLEN
+    peers = len(ring.offsets)
+    owner = zh == y
+
+    def by_x(own, other):
+        return jnp.where(x == c, own, other)
+
+    def regroup(prompt_rows, cont_rows):
+        cont_rows = cont_rows.reshape(local_conts * CLEN, half_d)
+        first = jnp.where(x == 0, prompt_rows, cont_rows)
+        second = jnp.where(x == 0, cont_rows, prompt_rows)
+        return ring.to_group(first, 0), ring.to_group(second, 1)
+
+    def feature_order(own, other):
+        def cut(value, place):
+            low = value[..., :part_d]
+            high = value[..., part_d:]
+            return jnp.where(c == place, low, high)
+
+        return jnp.concatenate([cut(own, 0), cut(other, 0), cut(own, 1), cut(other, 1)], axis=-1)
+
+    def natural_order(value):
+        pieces = [value[..., i * part_d : (i + 1) * part_d] for i in range(4)]
+        own_low = jnp.where(c == 0, pieces[0], pieces[2])
+        own_high = jnp.where(c == 0, pieces[2], pieces[0])
+        other_low = jnp.where(c == 0, pieces[1], pieces[3])
+        other_high = jnp.where(c == 0, pieces[3], pieces[1])
+        return own_low, own_high, other_low, other_high
+
+    got_a, got_b = regroup(x_prompt[0], x_cont[0])
+    own_valid = jnp.where(x == 0, prompt_valid.reshape(-1), cont_valid.reshape(-1))
+    small_in = jnp.concatenate([own_valid, segment_ids.reshape(-1), offsets.reshape(-1)])
+    small_len = small_in.shape[0]
+    small_pad = -small_len % LANES
+    small = ring.to_group(
+        jnp.concatenate([small_in, jnp.zeros((small_pad,), jnp.int32)]).reshape(-1, LANES), 0
+    ).reshape(-1)
+    validity = small[:local].astype(F32)
+    segment_row = small[local : local + PROMPT]
+    offset_row = small[local + PROMPT : local + PROMPT + CONTS]
+    tokens_b = feature_order(by_x(got_a, got_b), by_x(got_b, got_a))
+    tokens = tokens_b.astype(F32)
+
+    packed = jnp.concatenate(
+        [
+            w_forget.T.astype(F32),
+            first_gain[None].astype(F32),
+            second_gain[None].astype(F32),
+            jnp.pad(forget_bias, (0, half_d - heads))[None],
+        ],
+        axis=0,
+    )
+    packed_there = ring.swap(packed, "zh")
+    own_x = jnp.stack(
+        [jnp.where(zh == 0, packed, packed_there), jnp.where(zh == 0, packed_there, packed)]
+    )
+    other_x = ring.swap(own_x, "x")
+    both_x = feature_order(own_x, other_x)
+    gain_one = both_x[0, heads]
+    gain_two = both_x[0, heads + 1]
+
+    def head_slots(value):
+        first = jnp.where(y == 0, value[:, 0:2], value[:, 4:6])
+        slot_a = jnp.where(zh == 0, first[0], first[1])
+        slot_c = jnp.where(zh == 0, first[1], first[0])
+        slot_b = jnp.where(y == 0, value[0, 2:4], value[1, 2:4])
+        return jnp.concatenate([slot_a, slot_b, slot_c], axis=0)
+
+    forget_t = head_slots(both_x[:, :heads]).astype(BF)
+    bias_all = own_x[:, heads + 2, :heads]
+    bias_row = head_slots(bias_all[:, :, None])[:, 0]
+    bias_row = jnp.concatenate([bias_row, jnp.zeros((LANES - heads,), F32)])[None]
+    w_forget_all = jnp.concatenate(
+        [forget_t, jnp.zeros((LANES - heads, forget_t.shape[1]), BF)], axis=0
+    ).T
+
+    def rows_part(value):
+        return lax.dynamic_slice_in_dim(value, c * part_d, part_d, 0)
+
+    def cols_part(value):
+        return lax.dynamic_slice_in_dim(value, c * part_d, part_d, 1)
+
+    projections = [rows_part(w) for w in (w_query, w_outgate, w_key, w_value)]
+    first_pairs = jnp.concatenate(
+        [lax.dynamic_slice_in_dim(w, 2 * LANES * y, LANES, 1) for w in projections], axis=1
+    )
+    mid_pairs = jnp.concatenate([w[:, LANES : 2 * LANES] for w in projections], axis=1)
+    third_pairs = ring.swap(first_pairs, "zh")
+    mid_there = ring.swap(mid_pairs, "zh", lambda h: h["zh"] == h["y"])
+    mid_pairs = jnp.where(owner, mid_pairs, mid_there)
+
+    def whole_features(part):
+        half = jnp.concatenate([part, ring.swap(part, "x")], axis=0)
+        return jnp.concatenate([half, ring.swap(half, "c")], axis=0)
+
+    w_slots = [whole_features(part) for part in (first_pairs, mid_pairs, third_pairs)]
+    w_slots[0] = jnp.concatenate([w_slots[0], w_forget_all], axis=1)
+    third_pairs, w_out, w_down, w_gate, w_up = lax.optimization_barrier(
+        (third_pairs, w_out, w_down, w_gate, w_up)
+    )
+
+    out_part = cols_part(w_out)
+    down_part = lax.dynamic_slice_in_dim(cols_part(w_down), y * half_units, half_units, 0)
+    first_rows = lax.dynamic_slice_in_dim(out_part, 2 * LANES * y, LANES, 0)
+    mid_rows = out_part[LANES : 2 * LANES]
+    there = ring.swap(jnp.concatenate([first_rows, down_part], axis=0), "zh")
+    mid_rows_there = ring.swap(mid_rows, "zh", lambda h: h["zh"] == h["y"])
+    mid_rows = jnp.where(owner, mid_rows, mid_rows_there)
+    back_part = jnp.concatenate(
+        [first_rows, mid_rows, there[:LANES], down_part, there[LANES:]], axis=0
+    )
+    back_half = jnp.concatenate([back_part, ring.swap(back_part, "x")], axis=1)
+    back_all = jnp.concatenate([back_half, ring.swap(back_half, "c")], axis=1)
+    w_out_all = back_all[:width]
+    w_down_all = back_all[width:]
+
+    hidden_part = jnp.concatenate(
+        [
+            lax.dynamic_slice_in_dim(rows_part(w), y * half_units, half_units, 1)
+            for w in (w_gate, w_up)
+        ],
+        axis=1,
+    )
+    hidden_part = jnp.concatenate([hidden_part, ring.swap(hidden_part, "zh")], axis=1)
+    hidden_half = jnp.concatenate([hidden_part, ring.swap(hidden_part, "x")], axis=0)
+    w_hidden = jnp.concatenate([hidden_half, ring.swap(hidden_half, "c")], axis=0)
+
+    def chunk(value, k):
+        return value[k * local : (k + 1) * local]
+
+    dy_all = jnp.array([o[0] for o in ring.offsets], jnp.int32)
+    dz_all = jnp.array([o[1] for o in ring.offsets], jnp.int32)
+    places = ((y - dy_all) % 2) * zl_count + (zl - dz_all) % zl_count
+    unit_no = (places[:, None] * chunk_units + jnp.arange(chunk_units, dtype=jnp.int32)).reshape(-1)
+    natural = jnp.arange(pair_unit, dtype=jnp.int32)
+    pick = unit_no[:, None] == natural[None, :]
+    step = jnp.arange(CLEN, dtype=jnp.int32)
+    row_pos = (unit_no[:, None] * CLEN + step[None, :]).reshape(-1)
+    seg_rel = jnp.sum(
+        jnp.where(pick[:, :, None], segment_row.reshape(1, pair_unit, CLEN), 0), axis=1
+    )
+    offs_rel = jnp.sum(jnp.where(pick, offset_row[None, :], 0), axis=1)
+    last_rel = jnp.sum(
+        jnp.where(
+            jnp.arange(PROMPT, dtype=jnp.int32)[None, :] == offs_rel[:, None] - 1,
+            segment_row[None, :],
+            0,
+        ),
+        axis=1,
+    )
+    limit = jnp.where(c == 0, unit_no * CLEN, offs_rel)
+    doc_row = jnp.where(c == 0, seg_rel, last_rel[:, None]).reshape(-1, 1)
+    seg_col = seg_rel.reshape(-1, 1)
+    lane = jnp.arange(LANES, dtype=jnp.int32)[None, :]
+    unit_col = jnp.repeat(natural, CLEN)[:, None]
+    pieces = 3 * heads
+    is_doc = (lane >= DOC_LANE) & (lane < DOC_LANE + 4)
+    is_unit = (lane >= UNIT_LANE) & (lane < UNIT_LANE + pair_unit)
+    limit_lane = jnp.pad(limit, (UNIT_LANE, LANES - UNIT_LANE - pair_unit))[None, :]
+    q_base = jnp.where(
+        (lane >= FAR_PIECE) & (lane < FAR_PIECE + pieces),
+        1.0,
+        jnp.where(
+            (is_doc & (doc_row != lane - DOC_LANE)) | (is_unit & (unit_col == lane - UNIT_LANE)),
+            -NEVER,
+            0.0,
+        ),
+    ).astype(BF)
+    near_base = jnp.where(
+        (lane < pieces) | (is_doc & (doc_row == lane - DOC_LANE)), 1.0, 0.0
+    ).astype(BF)
+    far_base = jnp.where(
+        (lane < pieces)
+        | (is_doc & (seg_col == lane - DOC_LANE))
+        | (is_unit & (row_pos[:, None] >= limit_lane)),
+        1.0,
+        0.0,
+    ).astype(BF)
+    tri = (step[:, None] >= step[None, :]).astype(F32)
+    earlier = (unit_no[None, :] < unit_no[:, None]).astype(F32)
+    later = (unit_no[None, :] > unit_no[:, None]).astype(F32)
+    hot = (row_pos[None, :] == limit[:, None] - 1).astype(F32)
+    cont_hot = (row_pos[None, :] == offs_rel[:, None] - 1).astype(F32)
+
+    factor_one, scaled_one, normed_one = full_norm(tokens, gain_one)
+    normed_all = jnp.concatenate(ring.gather(normed_one), axis=0)
+    normed_all, teacher_prompt, teacher_cont = lax.optimization_barrier(
+        (normed_all, teacher_prompt, teacher_cont)
+    )
+    projects = [nn_dot(normed_all, w).astype(BF) for w in w_slots]
+    kv_there = [ring.swap(p[:, 2 * LANES :], "c") for p in projects]
+    forget_own = projects[0][:, 4 * LANES :]
+    forget_far = jnp.where(c == 0, forget_own, kv_there[0][:, 2 * LANES :])
+    flag = c.astype(jnp.int32).reshape(1)
+    teach_a, teach_b = regroup(teacher_prompt[0], teacher_cont[0])
+    head_lane = lane < heads
+
+    def keep_log(lin):
+        return jnp.where(head_lane, jax.nn.log_sigmoid(lin.astype(F32) + bias_row), 0.0)
+
+    def within(values, matrix):
+        return jnp.einsum(
+            "ts,ush->uth", matrix, values.reshape(pair_unit, CLEN, LANES), precision=highest
+        )
+
+    far_within = within(keep_log(forget_far), tri)
+    far_prefix = jnp.dot(earlier, far_within[:, -1], precision=highest)
+    cum_far = (far_within + far_prefix[:, None]).reshape(-1, LANES)
+    own_base = jnp.dot(hot, cum_far, precision=highest)
+    cum_near = (within(keep_log(forget_own), tri) + own_base[:, None]).reshape(-1, LANES)
+    gated, attended, logs = attend(
+        flag, projects, kv_there, cum_near, cum_far, q_base, near_base, far_base, local, heads
+    )
+    residual = tokens + ring.scatter_sum(lambda k: nn_dot(chunk(gated, k), w_out_all))
+    factor_two, scaled_two, normed_two = full_norm(residual, gain_two)
+    normed_two_all = jnp.concatenate(ring.gather(normed_two), axis=0)
+    gate_up = nn_dot(normed_two_all, w_hidden)
+
+    def split_units(value):
+        gate_rows = jnp.concatenate(
+            [value[:, :half_units], value[:, 2 * half_units : 3 * half_units]], axis=1
+        )
+        up_rows = jnp.concatenate(
+            [value[:, half_units : 2 * half_units], value[:, 3 * half_units :]], axis=1
+        )
+        return gate_rows, up_rows
+
+    gate_rows, up_rows = split_units(gate_up)
+    gate_sig = jax.nn.sigmoid(gate_rows)
+    silu_rows = gate_rows * gate_sig
+    hidden = (silu_rows * up_rows).astype(BF)
+    result = residual + ring.scatter_sum(lambda k: nn_dot(chunk(hidden, k), w_down_all))
+
+    teacher = feature_order(by_x(teach_a, teach_b), by_x(teach_b, teach_a)).astype(F32)
+    deviation = result - teacher
+    grad_result = validity[:, None] * deviation
+    error_own = 0.5 * jnp.sum(grad_result * deviation)
+    count_own = jnp.sum(validity)
+    grad_result_all = jnp.concatenate(ring.gather(grad_result.astype(BF)), axis=0)
+    grad_hid = nt_dot(grad_result_all, w_down_all)
+    grad_gate = (grad_hid * up_rows * gate_sig * (1.0 + gate_rows * (1.0 - gate_sig))).astype(BF)
+    grad_up = (grad_hid * silu_rows).astype(BF)
+    grad_gate_up = jnp.concatenate(
+        [
+            grad_gate[:, :half_units],
+            grad_up[:, :half_units],
+            grad_gate[:, half_units:],
+            grad_up[:, half_units:],
+        ],
+        axis=1,
+    )
+    grad_normed_two = ring.scatter_sum(lambda k: nt_dot(chunk(grad_gate_up, k), w_hidden))
+    grad_down_w = tn_dot(hidden, grad_result_all)
+    grad_hidden_w = tn_dot(normed_two_all, grad_gate_up)
+    gain_two_grad, grad_residual = full_norm_back(
+        grad_normed_two, factor_two, scaled_two, gain_two
+    )
+    grad_residual = grad_residual + grad_result
+    grad_residual_all = jnp.concatenate(ring.gather(grad_residual.astype(BF)), axis=0)
+    grad_gated = nt_dot(grad_residual_all, w_out_all)
+    grad_out_w = tn_dot(gated, grad_residual_all)
+    dqg, dkv_near, dkv_far, row_sum, near_sum, far_sum = attend_back(
+        flag,
+        projects,
+        kv_there,
+        cum_near,
+        cum_far,
+        q_base,
+        near_base,
+        far_base,
+        grad_gated,
+        attended,
+        logs,
+        local,
+        heads,
+    )
+    prompt_here = c == 0
+
+    def at_lane(value, first):
+        return jnp.pad(value[:, first : first + heads], ((0, 0), (0, LANES - heads)))
+
+    cum_grad = row_sum - at_lane(near_sum, FAR_PIECE)
+    unit_total = jnp.sum(cum_grad.reshape(pair_unit, CLEN, LANES), axis=1)
+    far_own = at_lane(far_sum, FAR_PIECE)
+    dkv_there = ring.swap(dkv_far.astype(BF), "c")
+    sums_there = ring.swap(jnp.concatenate([far_own, unit_total], axis=0), "c")
+    dkv = jnp.where(prompt_here, dkv_near + dkv_far + dkv_there.astype(F32), dkv_near).astype(BF)
+    total_rows = far_own.shape[0]
+    prompt_cum = (
+        cum_grad
+        - far_own
+        - sums_there[:total_rows]
+        + jnp.dot(cont_hot.T, sums_there[total_rows:], precision=highest)
+    )
+    cum_grad = jnp.where(prompt_here, prompt_cum, cum_grad)
+    log_within = within(cum_grad, tri.T)
+    log_suffix = jnp.where(prompt_here, jnp.dot(later, log_within[:, 0], precision=highest), 0.0)
+    log_grad = (log_within + log_suffix[:, None]).reshape(-1, LANES)
+    pre_grad = jnp.where(
+        head_lane, log_grad * jax.nn.sigmoid(-(forget_own.astype(F32) + bias_row)), 0.0
+    )
+    bias_grad = jnp.sum(pre_grad, axis=0)
+    grad_slots = []
+    for s in range(slots):
+        cols = slice(2 * s * LANES, 2 * (s + 1) * LANES)
+        grad_slots.append(jnp.concatenate([dqg[:, cols], dkv[:, cols]], axis=1))
+    forget_b = pre_grad.astype(BF)
+    project_grad = jnp.concatenate(grad_slots + [forget_b], axis=1)
+    w_project = jnp.concatenate(
+        [w_slots[0][:, : 4 * LANES], w_slots[1], w_slots[2], w_forget_all], axis=1
+    )
+    forget_gw = tn_dot(forget_b, normed_all)[:heads]
+
+    def low(value):
+        return lax.reduce_precision(value, 8, 7).astype(BF)
+
+    def outer_sum(value):
+        if ring.sizes["yo"] > 1:
+            return lax.psum(low(value), "yo").astype(F32)
+        return value
+
+    def fold(value, axis, dim):
+        size = value.shape[dim] // 2
+        mine = lax.slice_in_dim(value, 0, size, axis=dim)
+        theirs = lax.slice_in_dim(value, size, 2 * size, axis=dim)
+        return mine + ring.swap(theirs.astype(BF), axis).astype(F32)
+
+    def reduce_core_x(value, dim):
+        return fold(fold(value, "c", dim), "x", dim)
+
+    def both_parts(value, dim):
+        other = ring.swap(value, "c")
+        return jnp.concatenate(
+            [jnp.where(c == 0, value, other), jnp.where(c == 0, other, value)], axis=dim
+        )
+
+    def reduce_pairs(first, mid, third, dim):
+        first = first + ring.swap(third.astype(BF), "zh").astype(F32)
+        mid = mid + ring.swap(mid.astype(BF), "zh", lambda h: h["zh"] != h["y"]).astype(F32)
+        first = low(outer_sum(first))
+        mid = low(outer_sum(mid))
+        other = ring.swap(first, "y")
+        mid_other = ring.swap(mid, "y", lambda h: h["zh"] == h["y"])
+        mid = jnp.where(owner, mid, mid_other)
+        pair_low = jnp.where(y == 0, first, other)
+        pair_high = jnp.where(y == 0, other, first)
+        return [both_parts(v, dim) for v in (pair_low, mid, pair_high)]
+
+    def edge_sums(first, mid, third):
+        first = first + ring.swap(third.astype(BF), "zh").astype(F32)
+        mid = mid + ring.swap(mid.astype(BF), "zh", lambda h: h["zh"] != h["y"]).astype(F32)
+        return low(outer_sum(first)), low(outer_sum(mid))
+
+    down_mine = low(outer_sum(fold(reduce_core_x(grad_down_w, 1), "zh", 0)))
+    hid_mine = low(outer_sum(fold(reduce_core_x(grad_hidden_w, 0), "zh", 1)))
+    out_w = reduce_core_x(grad_out_w, 1)
+    out_first, out_mid = edge_sums(*[out_w[s * LANES : (s + 1) * LANES] for s in range(slots)])
+    rows_back, proj_all, gate_all, up_all, down_all, out_all, gain_all = last_step(
+        ring,
+        project_grad,
+        w_project,
+        normed_all,
+        tokens_b,
+        grad_residual,
+        gain_one[None],
+        hid_mine,
+        down_mine,
+        out_first,
+        out_mid,
+    )
+    gain_one_sum = gain_all[:, 0].reshape(-1)
+    projection_grads = [
+        jnp.concatenate(
+            [proj_all[:, (4 * s + i) * LANES : (4 * s + i + 1) * LANES] for s in range(slots)],
+            axis=1,
+        )
+        for i in range(4)
+    ]
+    forget_w = reduce_core_x(forget_gw, 1)
+    forget_grad = jnp.concatenate(
+        reduce_pairs(forget_w[0:2], forget_w[2:4], forget_w[4:6], 1), axis=0
+    ).T
+
+    def all_features(value):
+        own_low, own_high, other_low, other_high = natural_order(value)
+        own = jnp.concatenate([own_low, own_high], axis=-1)
+        other = jnp.concatenate([other_low, other_high], axis=-1)
+        return jnp.concatenate(
+            [jnp.where(x == 0, own, other), jnp.where(x == 0, other, own)], axis=-1
+        )
+
+    def place_heads(value):
+        slot_a, slot_b, slot_c = value[0:2], value[2:4], value[4:6]
+        blank = jnp.zeros_like(slot_a)
+        rows_out = []
+        for high in range(2):
+            is_own = zh == high
+            edge = jnp.where(is_own, slot_a, slot_c)
+            mid = jnp.where(y == high, slot_b, blank)
+            quarter = jnp.concatenate(
+                [jnp.where(y == 0, edge, blank), mid, jnp.where(y == 1, edge, blank)], axis=0
+            )
+            for low_z in range(zl_count):
+                rows_out.append(jnp.where(zl == low_z, quarter, jnp.zeros_like(quarter)))
+        return jnp.concatenate(rows_out, axis=0)
+
+    bias_place = place_heads(bias_grad[:heads, None])[:, 0]
+    scalars = jnp.concatenate([error_own[None], count_own[None], bias_place])
+    sums = ring.total(jnp.pad(scalars, (0, LANES - scalars.shape[0]))[None])[0]
+    gain_two_sum = ring.total(all_features(gain_two_grad).reshape(-1, LANES)).reshape(-1)
+    error_total = sums[0]
+    count_total = sums[1]
+    groups = ring.sizes["yo"] * ring.sizes["y"] * ring.sizes["c"]
+    grad_scale = groups * (PROMPT + CONTS * CLEN) / count_total
+    loss_value = error_total / (D * count_total)
+
+    def own_half(value):
+        return lax.dynamic_slice_in_dim(value, x * half_d, half_d, value.ndim - 1)
+
+    quarter_no = zh * zl_count + zl
+    bias_out = lax.dynamic_slice_in_dim(sums, 2 + quarter_no * heads, heads, 0)
+
+    def scaled(value):
+        return value.astype(F32) * grad_scale
+
+    return (
+        loss_value,
+        scaled(rows_back[0])[None],
+        scaled(rows_back[1]).reshape(1, local_conts, CLEN, half_d),
+        scaled(own_half(gain_one_sum)),
+        scaled(projection_grads[0]),
+        scaled(projection_grads[2]),
+        scaled(projection_grads[3]),
+        scaled(projection_grads[1]),
+        scaled(forget_grad),
+        scaled(bias_out),
+        scaled(out_all),
+        scaled(own_half(gain_two_sum)),
+        scaled(gate_all),
+        scaled(up_all),
+        scaled(down_all),
+    )
+
+
+def specs(dp, row, col):
     in_specs = (
-        P("dp", "col", "row"),
-        P("dp", "col", None, "row"),
-        P("dp", "col", "row"),
-        P("dp", "col", None, "row"),
-        P("dp", None),
-        P("dp", None),
-        P("dp", "col"),
-        P("dp", "col", None),
-        P("row"),
-        P("row", "col"),
-        P("row", "col"),
-        P("row", "col"),
-        P("row", "col"),
-        P("row", "col"),
-        P("col"),
-        P("col", "row"),
-        P("row"),
-        P("row", "col"),
-        P("row", "col"),
-        P("col", "row"),
+        P(dp, col, row),
+        P(dp, col, None, row),
+        P(dp, col, row),
+        P(dp, col, None, row),
+        P(dp, None),
+        P(dp, None),
+        P(dp, col),
+        P(dp, col, None),
+        P(row),
+        P(row, col),
+        P(row, col),
+        P(row, col),
+        P(row, col),
+        P(row, col),
+        P(col),
+        P(col, row),
+        P(row),
+        P(row, col),
+        P(row, col),
+        P(col, row),
     )
     out_specs = (
         P(),
-        P("dp", "col", "row"),
-        P("dp", "col", None, "row"),
-        P("row"),
-        P("row", "col"),
-        P("row", "col"),
-        P("row", "col"),
-        P("row", "col"),
-        P("row", "col"),
-        P("col"),
-        P("col", "row"),
-        P("row"),
-        P("row", "col"),
-        P("row", "col"),
-        P("col", "row"),
-    )
-    return jax.shard_map(body, mesh=mesh, in_specs=in_specs, out_specs=out_specs, check_vma=False)
+        P(dp, col, row),
+        P(dp, col, None, row),
+        P(row),
+        P(row, col),
+        P(row, col),
+        P(row, col),
+        P(row, col),
+        P(row, col),
+        P(col),
+        P(col, row),
+        P(row),
+        P(row, col),
+        P(row, col),
+        P(col, row),
+    )
+    return in_specs, out_specs
+
+
+def solution(mesh):
+    dp, row, col = mesh.shape["dp"], mesh.shape["row"], mesh.shape["col"]
+    heads = HEADS // col
+    if dp == 4 and row == 2 and col % 2 == 0 and heads == 6:
+        sizes = {"yo": dp // 4, "y": 2, "c": 2, "x": 2, "zh": 2, "zl": col // 2}
+        ring_mesh = Mesh(mesh.devices.reshape([sizes[a] for a in AX]), AX)
+        in_specs, out_specs = specs(("yo", "y", "c"), "x", ("zh", "zl"))
+        step = functools.partial(ring_body, Ring(sizes))
+        return jax.shard_map(
+            step, mesh=ring_mesh, in_specs=in_specs, out_specs=out_specs, check_vma=False
+        )
+    in_specs, out_specs = specs("dp", "row", "col")
+    return jax.shard_map(
+        wide_body, mesh=mesh, in_specs=in_specs, out_specs=out_specs, check_vma=False
+    )

time: 2120 us -> 874 us (0.41)
  waiting for transfers between devices: 1320 us -> 351 us
  blocking collectives: 303 us -> 0 us
  Pallas kernels: 0 us -> 183 us
  starting transfers between devices: 0.96 us -> 105 us
  matrix products: 171 us -> 70.2 us
  other arithmetic: 194 us -> 106 us
  local copies, waits for them, and re-layouts: 105 us -> 42.3 us
    unnamed x22 -> x0, waiting for transfers between devices: 624 us -> none
    all_gather x9 -> x0, waiting for transfers between devices: 431 us -> none  [the longest x4 241 us: group_rows(): return lax.all_gather(local_rows, 'col', axis=0, tiled=True)]
    ppermute x0 -> x77, waiting for transfers between devices: none -> 351 us  [move(): return lax.ppermute(value, AX, self.pairs(target, source_ok))]
    psum x8 -> x0, blocking collectives: 288 us -> none  [the longest x1 182 us: one_group(): kv_grad_full, cum_grad_full = lax.psum((kv_grad_part, cum_grad_part), 'row')]
    reduce_scatter x4 -> x0, waiting for transfers between devices: 229 us -> none  [token_sums(): lax.psum_scatter(partial_rows.astype(jnp.bfloat16), 'col', scatter_dimens...]
    pallas_call x0 -> x3, Pallas kernels: none -> 183 us  [the longest x1 132 us: last_step(): pl.pallas_call(functools.partial(last_kernel, ring), out_shape=(jax.Shape...]
    ppermute x0 -> x77, starting transfers between devices: none -> 105 us  [move(): return lax.ppermute(value, AX, self.pairs(target, source_ok))]
    dot_general x33 -> x29, matrix products: 161 us -> 70.2 us  [the longest x12 27.5 us: nn_dot(): return jnp.dot(left_op, right_op, preferred_element_type=F32)]
  transfers between devices with their start and end apart: 18 -> 77, of which waited for: 16 -> 37; matrix products, arithmetic and copies ran while one was open for 6% -> 19% of each run, Pallas kernels for 0% -> 6%
where the time goes in v1:
time: 874 us; the launch traced here: 864 us
  waiting for transfers between devices  351 us (40%)
  Pallas kernels  183 us (21%)
  other arithmetic  106 us (12%)
  starting transfers between devices  105 us (12%)
  matrix products  70.2 us (8%)
  local copies, waits for them, and re-layouts  42.3 us (5%)
    ppermute x77, waiting for transfers between devices, move(): return lax.ppermute(value, AX, self.pairs(target, source_ok))  351 us
    pallas_call x1, Pallas kernels, last_step(): pl.pallas_call(functools.partial(last_kernel, ring), out_shape=(jax.Shape...  132 us
    ppermute x77, starting transfers between devices, move(): return lax.ppermute(value, AX, self.pairs(target, source_ok))  105 us
    pallas_call x1, Pallas kernels, attend_back(): pl.pallas_call(functools.partial(attend_back_kernel, heads), grid=(steps,...  30.2 us
    dot_general x12, matrix products, nn_dot(): return jnp.dot(left_op, right_op, preferred_element_type=F32)  27.5 us
    concatenate x1, other arithmetic, ring_body(): jnp.concatenate([w_slots[0][:, :4 * LANES], w_slots[1], w_slots[2], w_for...  25.8 us
    dot_general x6, matrix products, nt_dot(): lax.dot_general(left_op, right_op, (((1,), (1,)), ((), ())), preferred_el...  22.1 us
    pallas_call x1, Pallas kernels, attend(): pl.pallas_call(functools.partial(attend_kernel, heads), grid=(steps,), ou...  20.7 us
  transfers between devices with their start and end apart: 77, of which 37 were waited for; matrix products, arithmetic and copies ran while one was open for 19% of the time, Pallas kernels for 6%

profile of v1, /device:TPU:0, one launch (start us, length us, event | category | flops | bytes accessed | tf_op | source)
XLA Modules:
  0.0 864.4 jit_solution(7768223288669727392)
XLA Ops:
  38.7 9.1 %collective-permute-done.2 = bf16[256,768]{1,0:T(8,128)(2,1)} collective-permute-done((bf16[256,768]{1,0:T(8,128)(2,1)}, bf16[256,768]{1,0:T(8,128)(2,1)}, u32[]{:S(2)}, u32[]{:S(2)}) %collective-permute-start.2) | collective-permute-done | bytes 393248 | tf_op jit(solution)/shard_map/ppermute | solution.py:605
  49.5 19.1 %collective-permute-start.7 = (bf16[256,1536]{1,0:T(8,128)(2,1)S(1)}, bf16[256,1536]{1,0:T(8,128)(2,1)S(1)}, u32[]{:S(2)}, u32[]{:S(2)}) collective-permute-start(bf16[256,1536]{1,0:T(8,128)(2,1)S(1)} %fusion.30), channel_id=1, source_target_pairs={{0,17},{1,16},{2,19},{3,18},{4,21},{5,20},{6,23},{7,22},{8,25},{9,... | collective-permute-start | bytes 2359304 | tf_op jit(solution)/shard_map/ppermute | solution.py:605
  82.0 5.2 collective-permute-done.19
  92.3 16.2 %collective-permute-done.20 = bf16[640,384]{1,0:T(8,128)(2,1)S(1)} collective-permute-done((bf16[640,384]{1,0:T(8,128)(2,1)S(1)}, bf16[640,384]{1,0:T(8,128)(2,1)S(1)}, u32[]{:S(2)}, u32[]{:S(2)}) %collective-permute-start.20) | collective-permute-done | bytes 491552 | tf_op jit(solution)/shard_map/ppermute | solution.py:605
  109.5 16.4 %collective-permute-done.5 = bf16[256,1536]{1,0:T(8,128)(2,1)S(1)} collective-permute-done((bf16[256,1536]{1,0:T(8,128)(2,1)S(1)}, bf16[256,1536]{1,0:T(8,128)(2,1)S(1)}, u32[]{:S(2)}, u32[]{:S(2)}) %collective-permute-start.5) | collective-permute-done | bytes 786464 | tf_op jit(solution)/shard_map/ppermute | solution.py:605
  129.3 12.7 %collective-permute-done.29 = bf16[384,1024]{1,0:T(8,128)(2,1)S(1)} collective-permute-done((bf16[384,1024]{1,0:T(8,128)(2,1)S(1)}, bf16[384,1024]{1,0:T(8,128)(2,1)S(1)}, u32[]{:S(2)}, u32[]{:S(2)}) %collective-permute-start.29) | collective-permute-done | bytes 786464 | tf_op jit(solution)/shard_map/ppermute | solution.py:605
  155.2 28.1 %collective-permute-done.30 = bf16[384,2048]{1,0:T(8,128)(2,1)S(1)} collective-permute-done((bf16[384,2048]{1,0:T(8,128)(2,1)S(1)}, bf16[384,2048]{1,0:T(8,128)(2,1)S(1)}, u32[]{:S(2)}, u32[]{:S(2)}) %collective-permute-start.30) | collective-permute-done | bytes 1572896 | tf_op jit(solution)/shard_map/ppermute | solution.py:605
  183.4 8.8 %pad_maximum_fusion.9 = bf16[768,2048]{1,0:T(8,128)(2,1)} fusion(bf16[384,2048]{1,0:T(8,128)(2,1)S(1)} %collective-permute-done.30, bf16[384,1024]{1,0:T(8,128)(2,1)S(1)} %collective-permute-done.29, bf16[384,512]{1,0:T(8,128)(2,1)S(1)} %dynamic_slice.63, bf16[384,512]{1,0:T(8,128)(2,1)S(1)} %dynamic_slice.62), kind=kLoop, calls=%fused_computation.20 | loop fusion | flops 12582912 | bytes 6291456 | tf_op jit(solution)/shard_map/concatenate | solution.py:1775
  192.2 20.7 %shard_map.325 = (bf16[1024,384]{1,0:T(8,128)(2,1)S(1)}, f32[1024,384]{1,0:T(8,128)}, f32[1024,128]{1,0:T(8,128)S(1)}) custom-call(s32[1]{0:T(128)} %bitcast.8.flag, bf16[1024,640]{1,0:T(8,128)(2,1)} %copy-done.53, bf16[1024,512]{1,0:T(8,128)(2,1)S(1)} %fusion.39.qg_b.near_b.own_b, bf16[1024,512]{1,0:T(8,128)(2,1)} %copy-done.66, ...), custom_call_target="tpu_custom_call" | custom-call | flops 6039797760 | bytes 7864320 | tf_op jit(solution)/shard_map/pallas_call | solution.py:875
  223.5 16.1 %collective-permute-done.23 = bf16[256,1536]{1,0:T(8,128)(2,1)S(1)} collective-permute-done((bf16[256,1536]{1,0:T(8,128)(2,1)S(1)}, bf16[256,1536]{1,0:T(8,128)(2,1)S(1)}, u32[]{:S(2)}, u32[]{:S(2)}) %collective-permute-start.23) | collective-permute-done | bytes 786464 | tf_op jit(solution)/shard_map/ppermute | solution.py:605
  239.6 30.9 %collective-permute-done.24 = bf16[256,1536]{1,0:T(8,128)(2,1)S(1)} collective-permute-done((bf16[256,1536]{1,0:T(8,128)(2,1)S(1)}, bf16[256,1536]{1,0:T(8,128)(2,1)S(1)}, u32[]{:S(2)}, u32[]{:S(2)}) %collective-permute-start.24) | collective-permute-done | bytes 786464 | tf_op jit(solution)/shard_map/ppermute | solution.py:605
  276.0 15.2 %pad_maximum_fusion = bf16[1536,2048]{1,0:T(8,128)(2,1)S(1)} fusion(bf16[768,2048]{1,0:T(8,128)(2,1)} %collective-permute-done.31, bf16[384,2048]{1,0:T(8,128)(2,1)S(1)} %collective-permute-done.30, bf16[384,1024]{1,0:T(8,128)(2,1)S(1)} %collective-permute-done.29, bf16[384,512]{1,0:T(8,128)(2,1)S(1)} %dynamic_slice.63, bf16[384,512]{1,0:T(8,128)(2,1)S(1)} %dynamic_slice.62), kind=kLoop, calls=%fused_computation.2 | loop fusion | flops 31457280 | bytes 12582912 | tf_op jit(solution)/shard_map/concatenate | solution.py:1776
  293.8 15.5 %collective-permute-done.27 = bf16[256,1536]{1,0:T(8,128)(2,1)S(1)} collective-permute-done((bf16[256,1536]{1,0:T(8,128)(2,1)S(1)}, bf16[256,1536]{1,0:T(8,128)(2,1)S(1)}, u32[]{:S(2)}, u32[]{:S(2)}) %collective-permute-start.27) | collective-permute-done | bytes 786464 | tf_op jit(solution)/shard_map/ppermute | solution.py:605
  311.1 6.7 fusion.51
  336.0 10.1 %collective-permute-done.32 = bf16[256,1536]{1,0:T(8,128)(2,1)S(1)} collective-permute-done((bf16[256,1536]{1,0:T(8,128)(2,1)S(1)}, bf16[256,1536]{1,0:T(8,128)(2,1)S(1)}, u32[]{:S(2)}, u32[]{:S(2)}) %collective-permute-start.32) | collective-permute-done | bytes 786464 | tf_op jit(solution)/shard_map/ppermute | solution.py:605
  346.1 18.8 %collective-permute-done.33 = bf16[256,1536]{1,0:T(8,128)(2,1)S(1)} collective-permute-done((bf16[256,1536]{1,0:T(8,128)(2,1)S(1)}, bf16[256,1536]{1,0:T(8,128)(2,1)S(1)}, u32[]{:S(2)}, u32[]{:S(2)}) %collective-permute-start.33) | collective-permute-done | bytes 786464 | tf_op jit(solution)/shard_map/ppermute | solution.py:605
  373.9 16.9 %collective-permute-done.39 = bf16[256,1536]{1,0:T(8,128)(2,1)} collective-permute-done((bf16[256,1536]{1,0:T(8,128)(2,1)}, bf16[256,1536]{1,0:T(8,128)(2,1)}, u32[]{:S(2)}, u32[]{:S(2)}) %collective-permute-start.39) | collective-permute-done | bytes 786464 | tf_op jit(solution)/shard_map/ppermute | solution.py:605
  390.8 14.4 %collective-permute-done.38 = bf16[256,1536]{1,0:T(8,128)(2,1)} collective-permute-done((bf16[256,1536]{1,0:T(8,128)(2,1)}, bf16[256,1536]{1,0:T(8,128)(2,1)}, u32[]{:S(2)}, u32[]{:S(2)}) %collective-permute-start.38) | collective-permute-done | bytes 786464 | tf_op jit(solution)/shard_map/ppermute | solution.py:605
  405.3 9.0 %multiply_convert_fusion.1 = (bf16[1024,1024]{1,0:T(8,128)(2,1)S(1)}, bf16[1024,1024]{1,0:T(8,128)(2,1)S(1)}) fusion(f32[1024,512]{1,0:T(8,128)} %copy-done.16, f32[1024,512]{1,0:T(8,128)} %copy-done.17, f32[1024,512]{1,0:T(8,128)} %copy-done.18, f32[1024,512]{1,0:T(8,128)} %copy-done.15, bf16[1408,768]{1,0:T(8,128)(2,1)} %collective-permute-done.22, ...), kind=kOutput, calls=%fused_computation.8 | convolution fusion | flops 3258974208 | bytes 20054016 | tf_op jit(solution)/shard_map/dot_general | solution.py:658
  427.5 25.8 %pad_maximum_fusion.1.weight_in = bf16[1536,1664]{1,0:T(8,128)(2,1)} fusion(bf16[1536,128]{1,0:T(8,128)(2,1)S(1)} %copy-done.41, bf16[1536,512]{1,0:T(8,128)(2,1)S(1)} %copy-done.29, bf16[768,512]{1,0:T(8,128)(2,1)S(1)} %copy-done.57, bf16[384,512]{1,0:T(8,128)(2,1)S(1)} %copy-done.45, bf16[384,512]{1,0:T(8,128)(2,1)S(1)} %broadcast_select_fusion, ...), kind=kLoop, calls=%fused_computation.3 | loop fusion | flops 56229888 | bytes 10223616 | tf_op jit(solution)/shard_map/concatenate | solution.py:1959
  453.3 7.9 collective-permute-done.41
  471.6 5.3 fusion.48
  478.5 11.2 %collective-permute-done.45 = bf16[256,1536]{1,0:T(8,128)(2,1)S(1)} collective-permute-done((bf16[256,1536]{1,0:T(8,128)(2,1)S(1)}, bf16[256,1536]{1,0:T(8,128)(2,1)S(1)}, u32[]{:S(2)}, u32[]{:S(2)}) %collective-permute-start.45) | collective-permute-done | bytes 786464 | tf_op jit(solution)/shard_map/ppermute | solution.py:605
  489.6 15.5 %collective-permute-done.44 = bf16[256,1536]{1,0:T(8,128)(2,1)S(1)} collective-permute-done((bf16[256,1536]{1,0:T(8,128)(2,1)S(1)}, bf16[256,1536]{1,0:T(8,128)(2,1)S(1)}, u32[]{:S(2)}, u32[]{:S(2)}) %collective-permute-start.44) | collective-permute-done | bytes 786464 | tf_op jit(solution)/shard_map/ppermute | solution.py:605
  510.5 30.2 %shard_map.326 = (bf16[1024,768]{1,0:T(8,128)(2,1)}, f32[1024,768]{1,0:T(8,128)}, f32[1024,768]{1,0:T(8,128)}, f32[1024,128]{1,0:T(8,128)}, f32[1024,128]{1,0:T(8,128)}, /*index=5*/f32[1024,128]{1,0:T(8,128)}) custom-call(s32[1]{0:T(128)} %bitcast.8.flag, bf16[1024,640]{1,0:T(8,128)(2,1)} %copy-done.53, bf16[1024,512]{1,0:T(8,128)(2,1)} %copy-done.2, ...), custom_call_target="tpu_custom_call" | custom-call | flops 18119393280 | bytes 15728640 | tf_op jit(solution)/shard_map/pallas_call | solution.py:1052
  544.3 9.4 %fusion.50 = f32[1536,2048]{1,0:T(8,128)S(1)} fusion(bf16[256,1536]{1,0:T(8,128)(2,1)} %copy-done.82, bf16[256,1536]{1,0:T(8,128)(2,1)} %copy-done.83, bf16[256,1536]{1,0:T(8,128)(2,1)} %copy-done.84, bf16[256,1536]{1,0:T(8,128)(2,1)} %copy-done.60, bf16[1024,512]{1,0:T(8,128)(2,1)} %copy-done.25, bf16[1024,512]{1,0:T(8,128)(2,1)S(1)} %get-tuple-element.98, ...), kind=kOutput, calls=%fused_computation.125 | convolution fusion | flops 6471811072 | bytes 19922944 | tf_op jit(solution)/shard_map/dot_general | solution.py:664
  577.0 15.7 %collective-permute-done.49 = f32[1,128]{1,0:T(1,128)S(1)} collective-permute-done((f32[1,128]{1,0:T(1,128)S(1)}, f32[1,128]{1,0:T(1,128)S(1)}, u32[]{:S(2)}, u32[]{:S(2)}) %collective-permute-start.49) | collective-permute-done | bytes 544 | tf_op jit(solution)/shard_map/ppermute | solution.py:605
  627.8 5.2 collective-permute-done.60
  642.6 9.6 %collective-permute-done.62 = bf16[128,384]{1,0:T(8,128)(2,1)S(1)} collective-permute-done((bf16[128,384]{1,0:T(8,128)(2,1)S(1)}, bf16[128,384]{1,0:T(8,128)(2,1)S(1)}, u32[]{:S(2)}, u32[]{:S(2)}) %collective-permute-start.62) | collective-permute-done | bytes 98336 | tf_op jit(solution)/shard_map/ppermute | solution.py:605
  659.3 17.6 %collective-permute-done.54 = bf16[384,2048]{1,0:T(8,128)(2,1)S(1)} collective-permute-done((bf16[384,2048]{1,0:T(8,128)(2,1)S(1)}, bf16[384,2048]{1,0:T(8,128)(2,1)S(1)}, u32[]{:S(2)}, u32[]{:S(2)}) %collective-permute-start.54) | collective-permute-done | bytes 1572896 | tf_op jit(solution)/shard_map/ppermute | solution.py:605
  681.2 31.4 %collective-permute-done.55 = bf16[384,1024]{1,0:T(8,128)(2,1)S(1)} collective-permute-done((bf16[384,1024]{1,0:T(8,128)(2,1)S(1)}, bf16[384,1024]{1,0:T(8,128)(2,1)S(1)}, u32[]{:S(2)}, u32[]{:S(2)}) %collective-permute-start.55) | collective-permute-done | bytes 786464 | tf_op jit(solution)/shard_map/ppermute | solution.py:605
  713.8 131.9 %shard_map.327 = (bf16[2,256,768]{2,1,0:T(8,128)(2,1)}, bf16[768,1536]{1,0:T(8,128)(2,1)}, bf16[768,1024]{1,0:T(8,128)(2,1)}, bf16[768,1024]{1,0:T(8,128)(2,1)},...) custom-call(bf16[1024,1664]{1,0:T(8,128)(2,1)} %convert_dynamic-update-slice_fusion.grads_in, ...), custom_call_target="tpu_custom_call" | custom-call | flops 9663676416 | bytes 41943040 | tf_op jit(solution)/shard_map/pallas_call | solution.py:1550
  (542 shorter events, 251.1 us)
Async XLA Ops:
  6.1 64.6 %collective-permute-start.13 = (bf16[384,512]{1,0:T(8,128)(2,1)}, bf16[384,512]{1,0:T(8,128)(2,1)S(1)}, u32[]{:S(2)}, u32[]{:S(2)}) collective-permute-start(bf16[384,512]{1,0:T(8,128)(2,1)} %pad_maximum_fusion.28), channel_id=1, source_target_pairs={{0,2},{1,3},{2,0},{3,1},{4,6},{5,7},{6,4},{7,5},{8,10},{9,11},{10,... | collective-permute-start | bytes 1179656 | tf_op jit(solution)/shard_map/ppermute | solution.py:605
  10.2 69.8 %collective-permute-start.8 = (bf16[384,512]{1,0:T(8,128)(2,1)}, bf16[384,512]{1,0:T(8,128)(2,1)S(1)}, u32[]{:S(2)}, u32[]{:S(2)}) collective-permute-start(bf16[384,512]{1,0:T(8,128)(2,1)} %pad_maximum_fusion.28), channel_id=1, source_target_pairs={{0,4},{1,5},{2,6},{3,7},{4,0},{5,1},{6,2},{7,3},{8,12},{9,13},{10,... | collective-permute-start | bytes 1179656 | tf_op jit(solution)/shard_map/ppermute | solution.py:605
  22.4 48.1 %collective-permute-start.10 = (bf16[384,512]{1,0:T(8,128)(2,1)}, bf16[384,512]{1,0:T(8,128)(2,1)}, u32[]{:S(2)}, u32[]{:S(2)}) collective-permute-start(bf16[384,512]{1,0:T(8,128)(2,1)} %pad_maximum_fusion.29), channel_id=1, source_target_pairs={{0,2},{1,3},{4,6},{5,7},{8,10},{9,11},{12,14},{13,15},{18,16},{19,... | collective-permute-start | bytes 1179656 | tf_op jit(solution)/shard_map/ppermute | solution.py:605
  49.5 59.3 %collective-permute-start.7 = (bf16[256,1536]{1,0:T(8,128)(2,1)S(1)}, bf16[256,1536]{1,0:T(8,128)(2,1)S(1)}, u32[]{:S(2)}, u32[]{:S(2)}) collective-permute-start(bf16[256,1536]{1,0:T(8,128)(2,1)S(1)} %fusion.30), channel_id=1, source_target_pairs={{0,17},{1,16},{2,19},{3,18},{4,21},{5,20},{6,23},{7,22},{8,25},{9,... | collective-permute-start | bytes 2359304 | tf_op jit(solution)/shard_map/ppermute | solution.py:605
  68.6 40.8 %collective-permute-start.6 = (bf16[256,1536]{1,0:T(8,128)(2,1)S(1)}, bf16[256,1536]{1,0:T(8,128)(2,1)S(1)}, u32[]{:S(2)}, u32[]{:S(2)}) collective-permute-start(bf16[256,1536]{1,0:T(8,128)(2,1)S(1)} %fusion.30), channel_id=1, source_target_pairs={{0,16},{1,17},{2,18},{3,19},{4,20},{5,21},{6,22},{7,23},{8,24},{9,... | collective-permute-start | bytes 2359304 | tf_op jit(solution)/shard_map/ppermute | solution.py:605
  90.7 35.2 %collective-permute-start.5 = (bf16[256,1536]{1,0:T(8,128)(2,1)S(1)}, bf16[256,1536]{1,0:T(8,128)(2,1)S(1)}, u32[]{:S(2)}, u32[]{:S(2)}) collective-permute-start(bf16[256,1536]{1,0:T(8,128)(2,1)S(1)} %fusion.30), channel_id=1, source_target_pairs={{0,1},{1,0},{2,3},{3,2},{4,5},{5,4},{6,7},{7,6},{8,9},{9,8},{10,11... | collective-permute-start | bytes 2359304 | tf_op jit(solution)/shard_map/ppermute | solution.py:605
  92.1 49.9 %collective-permute-start.29 = (bf16[384,1024]{1,0:T(8,128)(2,1)S(1)}, bf16[384,1024]{1,0:T(8,128)(2,1)S(1)}, u32[]{:S(2)}, u32[]{:S(2)}) collective-permute-start(bf16[384,1024]{1,0:T(8,128)(2,1)S(1)} %pad_maximum_fusion.19), channel_id=1, source_target_pairs={{0,2},{1,3},{2,0},{3,1},{4,6},{5,7},{6,4},{7,5},{8,10},{9,11},{10,... | collective-permute-start | bytes 2359304 | tf_op jit(solution)/shard_map/ppermute | solution.py:605
  108.8 34.6 %collective-permute-start.12 = (bf16[768,512]{1,0:T(8,128)(2,1)S(1)}, bf16[768,512]{1,0:T(8,128)(2,1)S(1)}, u32[]{:S(2)}, u32[]{:S(2)}) collective-permute-start(bf16[768,512]{1,0:T(8,128)(2,1)S(1)} %pad_maximum_fusion.17), channel_id=1, source_target_pairs={{0,8},{1,9},{2,10},{3,11},{4,12},{5,13},{6,14},{7,15},{8,0},{9,1},... | collective-permute-start | bytes 2359304 | tf_op jit(solution)/shard_map/ppermute | solution.py:605
  109.4 35.9 %collective-permute-start.15 = (bf16[768,512]{1,0:T(8,128)(2,1)S(1)}, bf16[768,512]{1,0:T(8,128)(2,1)S(1)}, u32[]{:S(2)}, u32[]{:S(2)}) collective-permute-start(bf16[768,512]{1,0:T(8,128)(2,1)S(1)} %pad_maximum_fusion.18), channel_id=1, source_target_pairs={{0,8},{1,9},{2,10},{3,11},{4,12},{5,13},{6,14},{7,15},{8,0},{9,1},... | collective-permute-start | bytes 2359304 | tf_op jit(solution)/shard_map/ppermute | solution.py:605
  142.2 41.2 %collective-permute-start.30 = (bf16[384,2048]{1,0:T(8,128)(2,1)S(1)}, bf16[384,2048]{1,0:T(8,128)(2,1)S(1)}, u32[]{:S(2)}, u32[]{:S(2)}) collective-permute-start(bf16[384,2048]{1,0:T(8,128)(2,1)S(1)} %pad_maximum_fusion.13), channel_id=1, source_target_pairs={{0,4},{1,5},{2,6},{3,7},{4,0},{5,1},{6,2},{7,3},{8,12},{9,13},{10,... | collective-permute-start | bytes 4718600 | tf_op jit(solution)/shard_map/ppermute | solution.py:605
  145.2 46.9 %collective-permute-start.17 = (bf16[1024,256]{1,0:T(8,128)(2,1)S(1)}, bf16[1024,256]{1,0:T(8,128)(2,1)S(1)}, u32[]{:S(2)}, u32[]{:S(2)}) collective-permute-start(bf16[1024,256]{1,0:T(8,128)(2,1)S(1)} %slice.599), channel_id=1, source_target_pairs={{0,8},{1,9},{2,10},{3,11},{4,12},{5,13},{6,14},{7,15},{8,0},{9,1},... | collective-permute-start | bytes 1572872 | tf_op jit(solution)/shard_map/ppermute | solution.py:605
  147.3 44.9 %collective-permute-start.18 = (bf16[1024,256]{1,0:T(8,128)(2,1)S(1)}, bf16[1024,256]{1,0:T(8,128)(2,1)S(1)}, u32[]{:S(2)}, u32[]{:S(2)}) collective-permute-start(bf16[1024,256]{1,0:T(8,128)(2,1)S(1)} %slice.600), channel_id=1, source_target_pairs={{0,8},{1,9},{2,10},{3,11},{4,12},{5,13},{6,14},{7,15},{8,0},{9,1},... | collective-permute-start | bytes 1572872 | tf_op jit(solution)/shard_map/ppermute | solution.py:605
  152.9 60.1 %collective-permute-start.22 = (bf16[1408,768]{1,0:T(8,128)(2,1)S(1)}, bf16[1408,768]{1,0:T(8,128)(2,1)}, u32[]{:S(2)}, u32[]{:S(2)}) collective-permute-start(bf16[1408,768]{1,0:T(8,128)(2,1)S(1)} %pad_maximum_fusion.12), channel_id=1, source_target_pairs={{0,8},{1,9},{2,10},{3,11},{4,12},{5,13},{6,14},{7,15},{8,0},{9,1},... | collective-permute-start | bytes 6488072 | tf_op jit(solution)/shard_map/ppermute | solution.py:605
  192.1 83.2 %collective-permute-start.31 = (bf16[768,2048]{1,0:T(8,128)(2,1)}, bf16[768,2048]{1,0:T(8,128)(2,1)}, u32[]{:S(2)}, u32[]{:S(2)}) collective-permute-start(bf16[768,2048]{1,0:T(8,128)(2,1)} %pad_maximum_fusion.9), channel_id=1, source_target_pairs={{0,8},{1,9},{2,10},{3,11},{4,12},{5,13},{6,14},{7,15},{8,0},{9,1},... | collective-permute-start | bytes 9437192 | tf_op jit(solution)/shard_map/ppermute | solution.py:605
  216.2 54.3 %collective-permute-start.24 = (bf16[256,1536]{1,0:T(8,128)(2,1)S(1)}, bf16[256,1536]{1,0:T(8,128)(2,1)S(1)}, u32[]{:S(2)}, u32[]{:S(2)}) collective-permute-start(bf16[256,1536]{1,0:T(8,128)(2,1)S(1)} %convolution_convert_fusion.7), channel_id=1, source_target_pairs={{0,16},{1,17},{2,18},{3,19},{4,20},{5,21},{6,22},{7,23},{8,24},{9,... | collective-permute-start | bytes 2359304 | tf_op jit(solution)/shard_map/ppermute | solution.py:605
  219.3 51.2 %collective-permute-start.25 = (bf16[256,1536]{1,0:T(8,128)(2,1)S(1)}, bf16[256,1536]{1,0:T(8,128)(2,1)S(1)}, u32[]{:S(2)}, u32[]{:S(2)}) collective-permute-start(bf16[256,1536]{1,0:T(8,128)(2,1)S(1)} %convolution_convert_fusion.6), channel_id=1, source_target_pairs={{0,17},{1,16},{2,19},{3,18},{4,21},{5,20},{6,23},{7,22},{8,25},{9,... | collective-permute-start | bytes 2359304 | tf_op jit(solution)/shard_map/ppermute | solution.py:605
  221.8 113.0 %collective-permute-start.35 = (bf16[256,768]{1,0:T(8,128)(2,1)}, bf16[256,768]{1,0:T(8,128)(2,1)S(1)}, u32[]{:S(2)}, u32[]{:S(2)}) collective-permute-start(bf16[256,768]{1,0:T(8,128)(2,1)} %get-tuple-element.108), channel_id=1, source_target_pairs={{0,0},{1,1},{2,16},{3,17},{4,8},{5,9},{6,24},{7,25},{8,2},{9,3},{1... | collective-permute-start | bytes 1179656 | tf_op jit(solution)/shard_map/ppermute | solution.py:605
  239.6 95.3 %collective-permute-start.36 = (bf16[256,768]{1,0:T(8,128)(2,1)}, bf16[256,768]{1,0:T(8,128)(2,1)}, u32[]{:S(2)}, u32[]{:S(2)}) collective-permute-start(bf16[256,768]{1,0:T(8,128)(2,1)} %get-tuple-element.109), channel_id=1, source_target_pairs={{0,8},{1,9},{2,24},{3,25},{4,0},{5,1},{6,16},{7,17},{8,10},{9,11},... | collective-permute-start | bytes 1179656 | tf_op jit(solution)/shard_map/ppermute | solution.py:605
  275.3 34.3 %collective-permute-start.26 = (bf16[256,1536]{1,0:T(8,128)(2,1)S(1)}, bf16[256,1536]{1,0:T(8,128)(2,1)S(1)}, u32[]{:S(2)}, u32[]{:S(2)}) collective-permute-start(bf16[256,1536]{1,0:T(8,128)(2,1)S(1)} %multiply_convert_fusion.4), channel_id=1, source_target_pairs={{0,1},{1,0},{2,3},{3,2},{4,5},{5,4},{6,7},{7,6},{8,9},{9,8},{10,11... | collective-permute-start | bytes 2359304 | tf_op jit(solution)/shard_map/ppermute | solution.py:605
  329.0 35.9 %collective-permute-start.33 = (bf16[256,1536]{1,0:T(8,128)(2,1)S(1)}, bf16[256,1536]{1,0:T(8,128)(2,1)S(1)}, u32[]{:S(2)}, u32[]{:S(2)}) collective-permute-start(bf16[256,1536]{1,0:T(8,128)(2,1)S(1)} %convolution_convert_fusion.4), channel_id=1, source_target_pairs={{0,16},{1,17},{2,18},{3,19},{4,20},{5,21},{6,22},{7,23},{8,24},{9,... | collective-permute-start | bytes 2359304 | tf_op jit(solution)/shard_map/ppermute | solution.py:605
  425.7 35.5 %collective-permute-start.41 = (bf16[256,1536]{1,0:T(8,128)(2,1)S(1)}, bf16[256,1536]{1,0:T(8,128)(2,1)S(1)}, u32[]{:S(2)}, u32[]{:S(2)}) collective-permute-start(bf16[256,1536]{1,0:T(8,128)(2,1)S(1)} %convolution_convert_fusion.1), channel_id=1, source_target_pairs={{0,16},{1,17},{2,18},{3,19},{4,20},{5,21},{6,22},{7,23},{8,24},{9,... | collective-permute-start | bytes 2359304 | tf_op jit(solution)/shard_map/ppermute | solution.py:605
  426.3 34.9 %collective-permute-start.42 = (bf16[256,1536]{1,0:T(8,128)(2,1)S(1)}, bf16[256,1536]{1,0:T(8,128)(2,1)S(1)}, u32[]{:S(2)}, u32[]{:S(2)}) collective-permute-start(bf16[256,1536]{1,0:T(8,128)(2,1)S(1)} %convolution_convert_fusion), channel_id=1, source_target_pairs={{0,17},{1,16},{2,19},{3,18},{4,21},{5,20},{6,23},{7,22},{8,25},{9,... | collective-permute-start | bytes 2359304 | tf_op jit(solution)/shard_map/ppermute | solution.py:605
  469.8 35.3 %collective-permute-start.44 = (bf16[256,1536]{1,0:T(8,128)(2,1)S(1)}, bf16[256,1536]{1,0:T(8,128)(2,1)S(1)}, u32[]{:S(2)}, u32[]{:S(2)}) collective-permute-start(bf16[256,1536]{1,0:T(8,128)(2,1)S(1)} %get-tuple-element.69), channel_id=1, source_target_pairs={{0,16},{1,17},{2,18},{3,19},{4,20},{5,21},{6,22},{7,23},{8,24},{9,... | collective-permute-start | bytes 2359304 | tf_op jit(solution)/shard_map/ppermute | solution.py:605
  470.9 34.4 %collective-permute-start.43 = (bf16[256,1536]{1,0:T(8,128)(2,1)S(1)}, bf16[256,1536]{1,0:T(8,128)(2,1)S(1)}, u32[]{:S(2)}, u32[]{:S(2)}) collective-permute-start(bf16[256,1536]{1,0:T(8,128)(2,1)S(1)} %get-tuple-element.69), channel_id=1, source_target_pairs={{0,1},{1,0},{2,3},{3,2},{4,5},{5,4},{6,7},{7,6},{8,9},{9,8},{10,11... | collective-permute-start | bytes 2359304 | tf_op jit(solution)/shard_map/ppermute | solution.py:605
  478.4 91.8 %collective-permute-start.56 = (bf16[1024,768]{1,0:T(8,128)(2,1)}, bf16[1024,768]{1,0:T(8,128)(2,1)}, u32[]{:S(2)}, u32[]{:S(2)}) collective-permute-start(bf16[1024,768]{1,0:T(8,128)(2,1)} %slice.867), channel_id=1, source_target_pairs={{0,8},{1,9},{2,10},{3,11},{4,12},{5,13},{6,14},{7,15},{8,0},{9,1},... | collective-permute-start | bytes 4718600 | tf_op jit(solution)/shard_map/ppermute | solution.py:605
  478.4 83.1 %collective-permute-start.75 = (f32[12,128]{1,0:T(8,128)S(1)}, f32[12,128]{1,0:T(8,128)S(1)}, u32[]{:S(2)}, u32[]{:S(2)}) collective-permute-start(f32[12,128]{1,0:T(8,128)S(1)} %add.426), channel_id=1, source_target_pairs={{0,2},{1,3},{2,0},{3,1},{4,6},{5,7},{6,4},{7,5},{8,10},{9,11},{10,... | collective-permute-start | bytes 18440 | tf_op jit(solution)/shard_map/ppermute | solution.py:605
  560.4 77.6 %collective-permute-start.53 = (bf16[768,2048]{1,0:T(8,128)(2,1)}, bf16[768,2048]{1,0:T(8,128)(2,1)}, u32[]{:S(2)}, u32[]{:S(2)}) collective-permute-start(bf16[768,2048]{1,0:T(8,128)(2,1)} %slice.866), channel_id=1, source_target_pairs={{0,8},{1,9},{2,10},{3,11},{4,12},{5,13},{6,14},{7,15},{8,0},{9,1},... | collective-permute-start | bytes 9437192 | tf_op jit(solution)/shard_map/ppermute | solution.py:605
  572.9 51.3 %collective-permute-start.57 = (bf16[1024,384]{1,0:T(8,128)(2,1)S(1)}, bf16[1024,384]{1,0:T(8,128)(2,1)S(1)}, u32[]{:S(2)}, u32[]{:S(2)}) collective-permute-start(bf16[1024,384]{1,0:T(8,128)(2,1)S(1)} %slice.869), channel_id=1, source_target_pairs={{0,4},{1,5},{2,6},{3,7},{4,0},{5,1},{6,2},{7,3},{8,12},{9,13},{10,... | collective-permute-start | bytes 2359304 | tf_op jit(solution)/shard_map/ppermute | solution.py:605
  576.9 46.8 %collective-permute-start.59 = (bf16[384,768]{1,0:T(8,128)(2,1)S(1)}, bf16[384,768]{1,0:T(8,128)(2,1)S(1)}, u32[]{:S(2)}, u32[]{:S(2)}) collective-permute-start(bf16[384,768]{1,0:T(8,128)(2,1)S(1)} %slice.871), channel_id=1, source_target_pairs={{0,8},{1,9},{2,10},{3,11},{4,12},{5,13},{6,14},{7,15},{8,0},{9,1},... | collective-permute-start | bytes 1769480 | tf_op jit(solution)/shard_map/ppermute | solution.py:605
  611.4 44.0 %collective-permute-start.52 = (bf16[1024,768]{1,0:T(8,128)(2,1)}, bf16[1024,768]{1,0:T(8,128)(2,1)}, u32[]{:S(2)}, u32[]{:S(2)}) collective-permute-start(bf16[1024,768]{1,0:T(8,128)(2,1)} %convert_element_type.324), channel_id=1, source_target_pairs={{0,8},{1,9},{2,10},{3,11},{4,12},{5,13},{6,14},{7,15},{8,0},{9,1},... | collective-permute-start | bytes 4718600 | tf_op jit(solution)/shard_map/ppermute | solution.py:605
  641.7 35.2 %collective-permute-start.54 = (bf16[384,2048]{1,0:T(8,128)(2,1)S(1)}, bf16[384,2048]{1,0:T(8,128)(2,1)S(1)}, u32[]{:S(2)}, u32[]{:S(2)}) collective-permute-start(bf16[384,2048]{1,0:T(8,128)(2,1)S(1)} %slice.868), channel_id=1, source_target_pairs={{0,4},{1,5},{2,6},{3,7},{4,0},{5,1},{6,2},{7,3},{8,12},{9,13},{10,... | collective-permute-start | bytes 4718600 | tf_op jit(solution)/shard_map/ppermute | solution.py:605
  677.5 35.2 %collective-permute-start.55 = (bf16[384,1024]{1,0:T(8,128)(2,1)S(1)}, bf16[384,1024]{1,0:T(8,128)(2,1)S(1)}, u32[]{:S(2)}, u32[]{:S(2)}) collective-permute-start(bf16[384,1024]{1,0:T(8,128)(2,1)S(1)} %slice.870), channel_id=1, source_target_pairs={{0,2},{1,3},{2,0},{3,1},{4,6},{5,7},{6,4},{7,5},{8,10},{9,11},{10,... | collective-permute-start | bytes 2359304 | tf_op jit(solution)/shard_map/ppermute | solution.py:605
  (141 other events, 3293.5 us)
